TPU v7x, 32 devices: a whole 2x2x4 slice. The times are simulated.
32 devices in a mesh: sub: 2 (over x), strip: 16 (over z, y, core).
Axes of the slice: x: 2, y: 2, z: 4, core: 2. Of those that a mesh axis runs over, the one named last changes fastest.
Arguments:
- forcing: float32 [2, 2048, 2048], P('sub', 'strip'), may hold values from -6 to 6
- mult_start: float32 [2, 2048, 2048], P('sub', 'strip'), may hold values from -6 to 6
- incr_start: float32 [2, 2048, 2048], P('sub', 'strip'), may hold values from -6 to 6
- diffusivity: float32 [2, 2048, 2048], P('sub', 'strip'), may hold values from 0.02 to 0.24
- north_corr: bfloat16 [2048, 2048], P('strip'), may hold values from -0.07629126 to 1.07629126
- east_corr: bfloat16 [2048, 2048], replicated, may hold values from -0.07629126 to 1.07629126
Outputs:
- mult_resid: float32 [2, 2048, 2048], P('sub', 'strip')
- grad_resid: float32 [2, 2048, 2048], P('sub', 'strip')
All inputs are finite; a program needn't handle non-finite values.
Results may differ from a plain program's by a relative error of at most 0.014.
Values may be sent and summed in bfloat16 or wider, within the bound.
No kernel may reach another device: no remote copies, remote signals or barrier semaphores. Data moves between devices by JAX's collectives and lax.ppermute only.
A program may use at most 128 MiB of HBM per device.

v0:
```python
import jax
import jax.numpy as jnp
from jax import lax
from jax.experimental import pallas as pl
from jax.experimental.pallas import tpu as pltpu
from jax.sharding import PartitionSpec as P


STEPS = 4
ITERS = 2

step_weight = 0.5
BOTH = ("sub", "strip")


def split_strip(size):
    core = 2 if size % 2 == 0 else 1
    chips = size // core
    outer = 4 if chips % 4 == 0 else 1
    return outer, chips // outer, core


def whole_step(forcing, mult_start, incr_start, diffusivity, north_corr, east_corr):
    forcing = forcing[0]
    diffuse = diffusivity[0]
    rows, cols = forcing.shape
    strips = lax.axis_size("strip")
    subs = lax.axis_size("sub")
    nz, ny, nk = split_strip(strips)
    width = cols // nz
    strip = lax.axis_index("strip")
    sub = lax.axis_index("sub")
    my_z, my_y, my_k = strip // (ny * nk), (strip // nk) % ny, strip % nk

    def send(value, move):
        pairs = []
        for s in range(subs):
            for t in range(strips):
                to = move(s, t)
                if to is not None:
                    pairs.append((s * strips + t, to[0] * strips + to[1]))
        return lax.ppermute(value, BOTH, pairs)

    def by_z(value, j):
        return send(value, lambda s, t: (s, t ^ (j * ny * nk)))

    def by_y(value, j):
        return send(value, lambda s, t: (s, t ^ (j * nk)))

    def by_k(value, j):
        return send(value, lambda s, t: (s, t ^ j))

    def to_strip(value, step):
        return send(value, lambda s, t: (s, t + step) if 0 <= t + step < strips else None)

    def to_sub(value, step):
        return send(value, lambda s, t: (s + step, t) if 0 <= s + step < subs else None)

    def xor_order(value, axis, index):
        size = value.shape[axis]
        bit = 1
        while bit < size:
            order = [i ^ bit for i in range(size)]
            flipped = jnp.concatenate(
                [lax.slice_in_dim(value, i, i + 1, axis=axis) for i in order], axis=axis
            )
            value = jnp.where((index // bit) % 2 == 1, flipped, value)
            bit *= 2
        return value

    half = rows // 2
    north_blocks = {0: (north_corr[:half], north_corr[half:])}
    bit = nz // 2
    while bit >= 1:
        for j, parts in list(north_blocks.items()):
            north_blocks[j ^ bit] = tuple(by_z(part, bit) for part in parts)
        bit //= 2
    north_rel = jnp.concatenate([part for j in range(nz) for part in north_blocks[j]], axis=0)

    def cut(low):
        return [lax.dynamic_slice_in_dim(low, (my_z ^ j) * width, width, axis=1) for j in range(nz)]

    def spread(own):
        side = 2 if nz % 2 == 0 else 1
        held = {0: own[0]}
        for j in [*range(side, nz), *range(1, side)]:
            held[j] = by_z(own[j], j)
        groups = {
            (0, 0, at // side): xor_order(
                jnp.stack([held[j] for j in range(at, at + side)]), 0, my_z % side
            )
            for at in range(0, nz, side)
        }
        for jy in range(1, ny):
            for i in range(nz // side):
                groups[0, jy, i] = by_y(groups[0, 0, i], jy)
        for jk in range(1, nk):
            for jy in range(ny):
                for i in range(nz // side):
                    groups[jk, jy, i] = by_k(groups[0, jy, i], jk)
        tall = jnp.zeros((nz, ny * nk, rows, width), jnp.bfloat16)
        for (jk, jy, i), group in groups.items():
            at = ((my_z // side) ^ i) * side, (my_y ^ jy) * nk + (my_k ^ jk), 0, 0
            tall = lax.dynamic_update_slice(tall, group[:, None], at)
        return tall.reshape(strips * rows, width)

    def product(tall):
        tile = jnp.dot(north_rel, tall, preferred_element_type=jnp.float32).astype(jnp.bfloat16)
        return [tile[j * rows : (j + 1) * rows] for j in range(nz)]

    def finish(tile):
        parts = [tile[0]] + [by_z(tile[j], j) for j in range(1, nz)]
        line = xor_order(jnp.stack(parts), 0, my_z).transpose(1, 0, 2).reshape(rows, cols)
        return jnp.dot(line, east_corr, preferred_element_type=jnp.float32)

    deep = 8
    tall_rows = rows + 2 * deep
    blocks = tall_rows // deep
    whole = pl.BlockSpec(memory_space=pltpu.VMEM)
    scalars = pl.BlockSpec(memory_space=pltpu.SMEM)
    limits = pltpu.CompilerParams(vmem_limit_bytes=20 * 1024 * 1024)
    f32, bf16 = jnp.float32, jnp.bfloat16
    wide_f32 = jax.ShapeDtypeStruct((tall_rows, cols), f32)
    field_f32 = jax.ShapeDtypeStruct((rows, cols), f32)
    field_bf16 = jax.ShapeDtypeStruct((rows, cols), bf16)
    ends = jnp.stack([strip > 0, strip < strips - 1, sub > 0]).astype(f32)

    def rows_at(block):
        return pl.ds(pl.multiple_of(block * deep, deep), deep)

    def laplace(source, block):
        here = source[rows_at(block + 1), :]
        row = lax.broadcasted_iota(jnp.int32, here.shape, 0)
        col = lax.broadcasted_iota(jnp.int32, here.shape, 1)
        above = pltpu.roll(jnp.where(row == deep - 1, source[rows_at(block), :], here), 1, 0)
        below = pltpu.roll(jnp.where(row == 0, source[rows_at(block + 2), :], here), deep - 1, 0)
        left = jnp.where(col == 0, 0.0, pltpu.roll(here, 1, 1))
        right = jnp.where(col == cols - 1, 0.0, pltpu.roll(here, cols - 1, 1))
        return above + below + left + right - 4.0 * here

    def kept(ends_ref, block):
        return jnp.where(block == 0, ends_ref[0], jnp.where(block == blocks - 1, ends_ref[1], 1.0))

    def clear_rims(buffer):
        zero = jnp.zeros((deep, cols), f32)
        for i in range(2):
            buffer[i, :deep, :] = zero
            buffer[i, tall_rows + deep :, :] = zero

    def adjoint_body(ends_ref, mult, above, below, coef, pulled, middle, buffer):
        clear_rims(buffer)
        pulled[:deep, :] = above[...].astype(f32)
        pulled[deep : rows + deep, :] = mult[...]
        pulled[rows + deep :, :] = below[...].astype(f32)

        def weigh(block, carry):
            at = rows_at(block)
            buffer[0, rows_at(block + 1), :] = coef[at, :] * pulled[at, :]
            return carry

        lax.fori_loop(0, blocks, weigh, 0)
        for step in range(STEPS):
            source, target = buffer.at[step % 2], buffer.at[(step + 1) % 2]

            def advance(block, carry):
                at = rows_at(block)
                value = (pulled[at, :] + laplace(source, block)) * kept(ends_ref, block)
                pulled[at, :] = value
                target[rows_at(block + 1), :] = coef[at, :] * value
                return carry

            lax.fori_loop(0, blocks, advance, 0)
        middle[...] = pulled[deep : rows + deep, :].astype(bf16)

    def adjoint(multiplier, above, below):
        return pl.pallas_call(
            adjoint_body,
            out_shape=[wide_f32, field_bf16],
            in_specs=[scalars] + [whole] * 4,
            out_specs=[whole] * 2,
            scratch_shapes=[pltpu.VMEM((2, tall_rows + 2 * deep, cols), f32)],
            compiler_params=limits,
            name="adjoint",
        )(ends, multiplier, above, below, diffuse_wide)

    def propagate(ends_ref, coef, buffer):
        for step in range(STEPS):
            source, target = buffer.at[step % 2], buffer.at[(step + 1) % 2]

            def advance(block, carry):
                at = rows_at(block)
                mid = rows_at(block + 1)
                target[mid, :] = (
                    source[mid, :] + coef[at, :] * laplace(source, block)
                ) * kept(ends_ref, block)
                return carry

            lax.fori_loop(0, blocks, advance, 0)
        return buffer[STEPS % 2, 2 * deep : rows + 2 * deep, :]

    def begin_body(ends_ref, coef, past, forcing_ref, incr, target, buffer):
        clear_rims(buffer)
        buffer[0, deep : tall_rows + deep, :] = past[...]
        target[...] = forcing_ref[...] - incr[...] + propagate(ends_ref, coef, buffer)

    def begin(past, incr):
        return pl.pallas_call(
            begin_body,
            out_shape=field_f32,
            in_specs=[scalars] + [whole] * 4,
            out_specs=whole,
            scratch_shapes=[pltpu.VMEM((2, tall_rows + 2 * deep, cols), f32)],
            compiler_params=limits,
            name="begin",
        )(ends, diffuse_wide, past, forcing, incr)

    def update_body(
        ends_ref, coef, past, arrived, pulled, mult, following, incr, forcing_ref,
        past_new, incr_new, target, grad, buffer
    ):
        clear_rims(buffer)
        past_new[...] = past[...] + step_weight * (
            arrived[...].astype(f32) - ends_ref[2] * pulled[...]
        )
        buffer[0, deep : tall_rows + deep, :] = past_new[...]
        slope = mult[...] - following[...].astype(f32)
        grad[...] = slope
        incr_new[...] = incr[...] + step_weight * slope
        target[...] = forcing_ref[...] - incr_new[...] + propagate(ends_ref, coef, buffer)

    def update(past, arrived, pulled, mult, following, incr):
        return pl.pallas_call(
            update_body,
            out_shape=[wide_f32, field_f32, field_f32, field_f32],
            in_specs=[scalars] + [whole] * 8,
            out_specs=[whole] * 4,
            scratch_shapes=[pltpu.VMEM((2, tall_rows + 2 * deep, cols), f32)],
            compiler_params=limits,
            name="update",
        )(ends, diffuse_wide, past, arrived, pulled, mult, following, incr, forcing)

    short = jnp.concatenate(
        [diffuse.astype(jnp.bfloat16), incr_start[0].astype(jnp.bfloat16)], axis=0
    )
    lowest = jnp.concatenate([short[rows - deep : rows], short[2 * rows - deep :]], axis=0)
    topmost = jnp.concatenate([short[:deep], short[rows : rows + deep]], axis=0)
    before = to_strip(lowest, 1)
    after = to_strip(topmost, -1)
    far = to_sub(short, 1).astype(f32)
    far_rims = to_sub(jnp.concatenate([before, after], axis=0), 1).astype(f32)
    diffuse_wide = jnp.concatenate(
        [far_rims[:deep], far[:rows], far_rims[2 * deep : 3 * deep]], axis=0
    )
    past_wide = jnp.concatenate(
        [far_rims[deep : 2 * deep], far[rows:], far_rims[3 * deep :]], axis=0
    )

    def advance(target, multiplier, incr, past_wide, tile):
        multiplier = multiplier + step_weight * (target - finish(tile))
        low = multiplier.astype(bf16)
        pieces = cut(low)
        above = to_strip(low[rows - deep :], 1)
        below = to_strip(low[:deep], -1)
        pulled, middle = adjoint(multiplier, above, below)
        following = to_sub(middle, -1)
        arrived = to_sub(jnp.concatenate([above, low, below], axis=0), 1)
        tile = product(spread(pieces))
        past_wide, incr, target, grad = update(
            past_wide, arrived, pulled, multiplier, following, incr
        )
        return target, multiplier, incr, past_wide, tile, grad

    multiplier = mult_start[0]
    incr = incr_start[0]
    tile = product(spread(cut(multiplier.astype(jnp.bfloat16))))
    target = begin(past_wide, incr)
    for _ in range(ITERS):
        target, multiplier, incr, past_wide, tile, grad = advance(
            target, multiplier, incr, past_wide, tile
        )
    mult_resid = target - finish(tile)
    return (mult_resid[None], grad[None])


def solution(mesh):
    return jax.shard_map(
        whole_step,
        mesh=mesh,
        in_specs=(
            P("sub", "strip", None),
            P("sub", "strip", None),
            P("sub", "strip", None),
            P("sub", "strip", None),
            P("strip", None),
            P(),
        ),
        out_specs=(P("sub", "strip", None), P("sub", "strip", None)),
        check_vma=False,
    )
```

profile of v0, /device:TPU:0, one launch (start us, length us, event | category | flops | bytes accessed | tf_op | source)
XLA Modules:
  0.0 213.0 jit_solution(12258279451781223524)
XLA Ops:
  0.6 2.0 fusion.17
  2.6 3.1 %collective-permute-start.4 = (bf16[64,2048]{1,0:T(8,128)(2,1)}, bf16[64,2048]{1,0:T(8,128)(2,1)}, u32[]{:S(2)}, u32[]{:S(2)}) collective-permute-start(bf16[64,2048]{1,0:T(8,128)(2,1)} %get-tuple-element.64), channel_id=1, source_target_pairs={{0,4},{1,5},{2,6},{3,7},{4,0},{5,1},{6,2},{7,3},{8,12},{9,13},{10,... | collective-permute-start | bytes 786440 | tf_op jit(solution)/shard_map/ppermute | solution.py:42
  5.6 2.6 %collective-permute-start.6 = (bf16[64,2048]{1,0:T(8,128)(2,1)}, bf16[64,2048]{1,0:T(8,128)(2,1)}, u32[]{:S(2)}, u32[]{:S(2)}) collective-permute-start(bf16[64,2048]{1,0:T(8,128)(2,1)} %get-tuple-element.64), channel_id=1, source_target_pairs={{0,8},{1,9},{2,10},{3,11},{4,12},{5,13},{6,14},{7,15},{8,0},{9,1},... | collective-permute-start | bytes 786440 | tf_op jit(solution)/shard_map/ppermute | solution.py:42
  16.8 8.9 %collective-permute-start.11 = (bf16[128,512]{1,0:T(8,128)(2,1)}, bf16[128,512]{1,0:T(8,128)(2,1)S(1)}, u32[]{:S(2)}, u32[]{:S(2)}) collective-permute-start(bf16[128,512]{1,0:T(8,128)(2,1)} %get-tuple-element.60), channel_id=1, source_target_pairs={{0,12},{1,13},{2,14},{3,15},{4,8},{5,9},{6,10},{7,11},{8,4},{9,5},... | collective-permute-start | bytes 393224 | tf_op jit(solution)/shard_map/ppermute | solution.py:42
  27.3 3.0 %collective-permute-done.11 = bf16[128,512]{1,0:T(8,128)(2,1)S(1)} collective-permute-done((bf16[128,512]{1,0:T(8,128)(2,1)}, bf16[128,512]{1,0:T(8,128)(2,1)S(1)}, u32[]{:S(2)}, u32[]{:S(2)}) %collective-permute-start.11) | collective-permute-done | bytes 131104 | tf_op jit(solution)/shard_map/ppermute | solution.py:42
  30.3 3.3 %collective-permute-start.7 = (bf16[64,2048]{1,0:T(8,128)(2,1)}, bf16[64,2048]{1,0:T(8,128)(2,1)S(1)}, u32[]{:S(2)}, u32[]{:S(2)}) collective-permute-start(bf16[64,2048]{1,0:T(8,128)(2,1)} %get-tuple-element.63), channel_id=1, source_target_pairs={{0,8},{1,9},{2,10},{3,11},{4,12},{5,13},{6,14},{7,15},{8,0},{9,1},... | collective-permute-start | bytes 786440 | tf_op jit(solution)/shard_map/ppermute | solution.py:42
  33.6 5.0 %collective-permute-done.12 = bf16[128,512]{1,0:T(8,128)(2,1)S(1)} collective-permute-done((bf16[128,512]{1,0:T(8,128)(2,1)}, bf16[128,512]{1,0:T(8,128)(2,1)S(1)}, u32[]{:S(2)}, u32[]{:S(2)}) %collective-permute-start.12) | collective-permute-done | bytes 131104 | tf_op jit(solution)/shard_map/ppermute | solution.py:42
  38.5 3.5 %collective-permute-start.3 = (bf16[256,2048]{1,0:T(8,128)(2,1)S(1)}, bf16[256,2048]{1,0:T(8,128)(2,1)S(1)}, u32[]{:S(2)}, u32[]{:S(2)}) collective-permute-start(bf16[256,2048]{1,0:T(8,128)(2,1)S(1)} %pad_maximum_fusion.2), channel_id=1, source_target_pairs={{0,16},{1,17},{2,18},{3,19},{4,20},{5,21},{6,22},{7,23},{8,24},{9,... | collective-permute-start | bytes 3145736 | tf_op jit(solution)/shard_map/ppermute | solution.py:42
  45.8 2.1 collective-permute-start.14
  48.0 5.0 %collective-permute-done.13 = bf16[2,128,512]{2,1,0:T(8,128)(2,1)S(1)} collective-permute-done((bf16[2,128,512]{2,1,0:T(8,128)(2,1)S(1)}, bf16[2,128,512]{2,1,0:T(8,128)(2,1)S(1)}, u32[]{:S(2)}, u32[]{:S(2)}) %collective-permute-start.13) | collective-permute-done | bytes 262176 | tf_op jit(solution)/shard_map/ppermute | solution.py:42
  53.0 3.7 %collective-permute-done.14 = bf16[2,128,512]{2,1,0:T(8,128)(2,1)S(1)} collective-permute-done((bf16[2,128,512]{2,1,0:T(8,128)(2,1)S(1)}, bf16[2,128,512]{2,1,0:T(8,128)(2,1)S(1)}, u32[]{:S(2)}, u32[]{:S(2)}) %collective-permute-start.14) | collective-permute-done | bytes 262176 | tf_op jit(solution)/shard_map/ppermute | solution.py:42
  56.8 2.1 collective-permute-start.9
  59.0 7.1 %collective-permute-done.8 = bf16[64,2048]{1,0:T(8,128)(2,1)S(1)} collective-permute-done((bf16[64,2048]{1,0:T(8,128)(2,1)}, bf16[64,2048]{1,0:T(8,128)(2,1)S(1)}, u32[]{:S(2)}, u32[]{:S(2)}) %collective-permute-start.8) | collective-permute-done | bytes 262176 | tf_op jit(solution)/shard_map/ppermute | solution.py:42
  66.1 2.9 %collective-permute-done.9 = bf16[64,2048]{1,0:T(8,128)(2,1)S(1)} collective-permute-done((bf16[64,2048]{1,0:T(8,128)(2,1)S(1)}, bf16[64,2048]{1,0:T(8,128)(2,1)S(1)}, u32[]{:S(2)}, u32[]{:S(2)}) %collective-permute-start.9) | collective-permute-done | bytes 262176 | tf_op jit(solution)/shard_map/ppermute | solution.py:42
  74.1 3.4 %collective-permute-done.19 = bf16[128,512]{0,1:T(8,128)(2,1)S(1)} collective-permute-done((bf16[128,512]{0,1:T(8,128)(2,1)S(1)}, bf16[128,512]{0,1:T(8,128)(2,1)S(1)}, u32[]{:S(2)}, u32[]{:S(2)}) %collective-permute-start.19) | collective-permute-done | bytes 131104 | tf_op jit(solution)/shard_map/ppermute | solution.py:42
  79.4 4.9 %collective-permute-done.21 = bf16[128,512]{0,1:T(8,128)(2,1)S(1)} collective-permute-done((bf16[128,512]{0,1:T(8,128)(2,1)S(1)}, bf16[128,512]{0,1:T(8,128)(2,1)S(1)}, u32[]{:S(2)}, u32[]{:S(2)}) %collective-permute-start.21) | collective-permute-done | bytes 131104 | tf_op jit(solution)/shard_map/ppermute | solution.py:42
  87.3 8.7 %begin.1 = f32[128,2048]{1,0:T(8,128)S(1)} custom-call(f32[3]{0:T(128)S(1)} %add_convert_fusion.ends_ref, f32[144,2048]{1,0:T(8,128)S(1)} %get-tuple-element.73.coef, f32[144,2048]{1,0:T(8,128)S(1)} %get-tuple-element.74.past, f32[128,2048]{1,0:T(8,128)S(1)} %bitcast.160, f32[128,2048]{1,0:T(8,128)S(1)} %bitcast.163), custom_call_target="tpu_custom_call" | custom-call | tf_op jit(solution)/shard_map/begin/pallas_call | solution.py:207
  99.1 5.4 %collective-permute-start.27 = (bf16[128,512]{1,0:T(8,128)(2,1)S(1)}, bf16[128,512]{1,0:T(8,128)(2,1)S(1)}, u32[]{:S(2)}, u32[]{:S(2)}) collective-permute-start(bf16[128,512]{1,0:T(8,128)(2,1)S(1)} %get-tuple-element.47), channel_id=1, source_target_pairs={{0,12},{1,13},{2,14},{3,15},{4,8},{5,9},{6,10},{7,11},{8,4},{9,5},... | collective-permute-start | bytes 393224 | tf_op jit(solution)/shard_map/ppermute | solution.py:42
  105.1 8.7 %adjoint.2 = (f32[144,2048]{1,0:T(8,128)S(1)}, bf16[128,2048]{1,0:T(8,128)(2,1)S(1)}) custom-call(f32[3]{0:T(128)S(1)} %add_convert_fusion.ends_ref, f32[128,2048]{1,0:T(8,128)S(1)} %get-tuple-element.23.mult, bf16[8,2048]{1,0:T(8,128)(2,1)S(1)} %collective-permute-done.22.above, bf16[8,2048]{1,0:T(8,128)(2,1)S(1)} %collective-permute-done.23.below, ...), custom_call_target="tpu_custom_call" | custom-call | tf_op jit(solution)/shard_map/adjoint/pallas_call | solution.py:176
  115.1 4.8 %collective-permute-start.24 = (bf16[144,2048]{1,0:T(8,128)(2,1)S(1)}, bf16[144,2048]{1,0:T(8,128)(2,1)S(1)}, u32[]{:S(2)}, u32[]{:S(2)}) collective-permute-start(bf16[144,2048]{1,0:T(8,128)(2,1)S(1)} %pad_maximum_fusion.3), channel_id=1, source_target_pairs={{0,16},{1,17},{2,18},{3,19},{4,20},{5,21},{6,22},{7,23},{8,24},{9,... | collective-permute-start | bytes 1769480 | tf_op jit(solution)/shard_map/ppermute | solution.py:42
  120.0 3.1 %collective-permute-start.29 = (bf16[2,128,512]{2,1,0:T(8,128)(2,1)S(1)}, bf16[2,128,512]{2,1,0:T(8,128)(2,1)S(1)}, u32[]{:S(2)}, u32[]{:S(2)}) collective-permute-start(bf16[2,128,512]{2,1,0:T(8,128)(2,1)S(1)} %maximum_select_fusion.12), channel_id=1, source_target_pairs={{0,2},{1,3},{2,0},{3,1},{4,6},{5,7},{6,4},{7,5},{8,10},{9,11},{10,... | collective-permute-start | bytes 786440 | tf_op jit(solution)/shard_map/ppermute | solution.py:42
  123.6 6.6 %collective-permute-done.29 = bf16[2,128,512]{2,1,0:T(8,128)(2,1)S(1)} collective-permute-done((bf16[2,128,512]{2,1,0:T(8,128)(2,1)S(1)}, bf16[2,128,512]{2,1,0:T(8,128)(2,1)S(1)}, u32[]{:S(2)}, u32[]{:S(2)}) %collective-permute-start.29) | collective-permute-done | bytes 262176 | tf_op jit(solution)/shard_map/ppermute | solution.py:42
  130.2 3.6 %collective-permute-done.30 = bf16[2,128,512]{2,1,0:T(8,128)(2,1)S(1)} collective-permute-done((bf16[2,128,512]{2,1,0:T(8,128)(2,1)S(1)}, bf16[2,128,512]{2,1,0:T(8,128)(2,1)S(1)}, u32[]{:S(2)}, u32[]{:S(2)}) %collective-permute-start.30) | collective-permute-done | bytes 262176 | tf_op jit(solution)/shard_map/ppermute | solution.py:42
  140.8 10.1 %update.2 = (f32[144,2048]{1,0:T(8,128)S(1)}, f32[128,2048]{1,0:T(8,128)S(1)}, f32[128,2048]{1,0:T(8,128)S(1)}, f32[128,2048]{1,0:T(8,128)}) custom-call(f32[3]{0:T(128)S(1)} %add_convert_fusion.ends_ref, f32[144,2048]{1,0:T(8,128)S(1)} %get-tuple-element.73.coef, f32[144,2048]{1,0:T(8,128)S(1)} %get-tuple-element.74.past, ...), custom_call_target="tpu_custom_call" | custom-call | tf_op jit(solution)/shard_map/update/pallas_call | solution.py:232
  157.1 5.9 %collective-permute-start.43 = (bf16[128,512]{1,0:T(8,128)(2,1)S(1)}, bf16[128,512]{1,0:T(8,128)(2,1)S(1)}, u32[]{:S(2)}, u32[]{:S(2)}) collective-permute-start(bf16[128,512]{1,0:T(8,128)(2,1)S(1)} %get-tuple-element.34), channel_id=1, source_target_pairs={{0,12},{1,13},{2,14},{3,15},{4,8},{5,9},{6,10},{7,11},{8,4},{9,5},... | collective-permute-start | bytes 393224 | tf_op jit(solution)/shard_map/ppermute | solution.py:42
  163.6 8.7 %adjoint.3 = (f32[144,2048]{1,0:T(8,128)S(1)}, bf16[128,2048]{1,0:T(8,128)(2,1)S(1)}) custom-call(f32[3]{0:T(128)S(1)} %add_convert_fusion.ends_ref, f32[128,2048]{1,0:T(8,128)S(1)} %get-tuple-element.21.mult, bf16[8,2048]{1,0:T(8,128)(2,1)S(1)} %collective-permute-done.38.above, bf16[8,2048]{1,0:T(8,128)(2,1)S(1)} %collective-permute-done.39.below, ...), custom_call_target="tpu_custom_call" | custom-call | tf_op jit(solution)/shard_map/adjoint/pallas_call | solution.py:176
  173.6 4.8 %collective-permute-start.40 = (bf16[144,2048]{1,0:T(8,128)(2,1)S(1)}, bf16[144,2048]{1,0:T(8,128)(2,1)S(1)}, u32[]{:S(2)}, u32[]{:S(2)}) collective-permute-start(bf16[144,2048]{1,0:T(8,128)(2,1)S(1)} %pad_maximum_fusion.4), channel_id=1, source_target_pairs={{0,16},{1,17},{2,18},{3,19},{4,20},{5,21},{6,22},{7,23},{8,24},{9,... | collective-permute-start | bytes 1769480 | tf_op jit(solution)/shard_map/ppermute | solution.py:42
  178.5 2.1 collective-permute-start.45
  181.2 6.6 %collective-permute-done.45 = bf16[2,128,512]{2,1,0:T(8,128)(2,1)S(1)} collective-permute-done((bf16[2,128,512]{2,1,0:T(8,128)(2,1)S(1)}, bf16[2,128,512]{2,1,0:T(8,128)(2,1)S(1)}, u32[]{:S(2)}, u32[]{:S(2)}) %collective-permute-start.45) | collective-permute-done | bytes 262176 | tf_op jit(solution)/shard_map/ppermute | solution.py:42
  187.8 3.6 %collective-permute-done.46 = bf16[2,128,512]{2,1,0:T(8,128)(2,1)S(1)} collective-permute-done((bf16[2,128,512]{2,1,0:T(8,128)(2,1)S(1)}, bf16[2,128,512]{2,1,0:T(8,128)(2,1)S(1)}, u32[]{:S(2)}, u32[]{:S(2)}) %collective-permute-start.46) | collective-permute-done | bytes 262176 | tf_op jit(solution)/shard_map/ppermute | solution.py:42
  195.4 2.9 %collective-permute-start.52 = (bf16[128,512]{0,1:T(8,128)(2,1)S(1)}, bf16[128,512]{0,1:T(8,128)(2,1)S(1)}, u32[]{:S(2)}, u32[]{:S(2)}) collective-permute-start(bf16[128,512]{0,1:T(8,128)(2,1)S(1)} %get-tuple-element.30), channel_id=1, source_target_pairs={{0,12},{1,13},{2,14},{3,15},{4,8},{5,9},{6,10},{7,11},{8,4},{9,5},... | collective-permute-start | bytes 393224 | tf_op jit(solution)/shard_map/ppermute | solution.py:42
  198.3 10.9 %update.3 = (f32[144,2048]{1,0:T(8,128)}, f32[128,2048]{1,0:T(8,128)}, f32[128,2048]{1,0:T(8,128)S(1)}, f32[128,2048]{1,0:T(8,128)}) custom-call(f32[3]{0:T(128)S(1)} %add_convert_fusion.ends_ref, f32[144,2048]{1,0:T(8,128)S(1)} %get-tuple-element.73.coef, f32[144,2048]{1,0:T(8,128)S(1)} %get-tuple-element.13.past, ...), custom_call_target="tpu_custom_call" | custom-call | tf_op jit(solution)/shard_map/update/pallas_call | solution.py:232
  (181 shorter events, 52.3 us)
Async XLA Ops:
  2.6 39.8 %collective-permute-start.4 = (bf16[64,2048]{1,0:T(8,128)(2,1)}, bf16[64,2048]{1,0:T(8,128)(2,1)}, u32[]{:S(2)}, u32[]{:S(2)}) collective-permute-start(bf16[64,2048]{1,0:T(8,128)(2,1)} %get-tuple-element.64), channel_id=1, source_target_pairs={{0,4},{1,5},{2,6},{3,7},{4,0},{5,1},{6,2},{7,3},{8,12},{9,13},{10,... | collective-permute-start | bytes 786440 | tf_op jit(solution)/shard_map/ppermute | solution.py:42
  5.6 39.1 %collective-permute-start.6 = (bf16[64,2048]{1,0:T(8,128)(2,1)}, bf16[64,2048]{1,0:T(8,128)(2,1)}, u32[]{:S(2)}, u32[]{:S(2)}) collective-permute-start(bf16[64,2048]{1,0:T(8,128)(2,1)} %get-tuple-element.64), channel_id=1, source_target_pairs={{0,8},{1,9},{2,10},{3,11},{4,12},{5,13},{6,14},{7,15},{8,0},{9,1},... | collective-permute-start | bytes 786440 | tf_op jit(solution)/shard_map/ppermute | solution.py:42
  10.4 16.2 %collective-permute-start.10 = (bf16[128,512]{1,0:T(8,128)(2,1)}, bf16[128,512]{1,0:T(8,128)(2,1)S(1)}, u32[]{:S(2)}, u32[]{:S(2)}) collective-permute-start(bf16[128,512]{1,0:T(8,128)(2,1)} %get-tuple-element.62), channel_id=1, source_target_pairs={{0,4},{1,5},{2,6},{3,7},{4,0},{5,1},{6,2},{7,3},{8,12},{9,13},{10,... | collective-permute-start | bytes 393224 | tf_op jit(solution)/shard_map/ppermute | solution.py:42
  14.2 11.5 %collective-permute-start.1 = (bf16[16,2048]{1,0:T(8,128)(2,1)}, bf16[16,2048]{1,0:T(8,128)(2,1)}, u32[]{:S(2)}, u32[]{:S(2)}) collective-permute-start(bf16[16,2048]{1,0:T(8,128)(2,1)} %pad_maximum_fusion.7), channel_id=1, source_target_pairs={{1,0},{2,1},{3,2},{4,3},{5,4},{6,5},{7,6},{8,7},{9,8},{10,9},{11,1... | collective-permute-start | bytes 196616 | tf_op jit(solution)/shard_map/ppermute | solution.py:42
  16.8 13.5 %collective-permute-start.11 = (bf16[128,512]{1,0:T(8,128)(2,1)}, bf16[128,512]{1,0:T(8,128)(2,1)S(1)}, u32[]{:S(2)}, u32[]{:S(2)}) collective-permute-start(bf16[128,512]{1,0:T(8,128)(2,1)} %get-tuple-element.60), channel_id=1, source_target_pairs={{0,12},{1,13},{2,14},{3,15},{4,8},{5,9},{6,10},{7,11},{8,4},{9,5},... | collective-permute-start | bytes 393224 | tf_op jit(solution)/shard_map/ppermute | solution.py:42
  25.7 12.8 %collective-permute-start.12 = (bf16[128,512]{1,0:T(8,128)(2,1)}, bf16[128,512]{1,0:T(8,128)(2,1)S(1)}, u32[]{:S(2)}, u32[]{:S(2)}) collective-permute-start(bf16[128,512]{1,0:T(8,128)(2,1)} %get-tuple-element.59), channel_id=1, source_target_pairs={{0,8},{1,9},{2,10},{3,11},{4,12},{5,13},{6,14},{7,15},{8,0},{9,1},... | collective-permute-start | bytes 393224 | tf_op jit(solution)/shard_map/ppermute | solution.py:42
  26.6 18.1 %collective-permute-start.5 = (bf16[64,2048]{1,0:T(8,128)(2,1)}, bf16[64,2048]{1,0:T(8,128)(2,1)S(1)}, u32[]{:S(2)}, u32[]{:S(2)}) collective-permute-start(bf16[64,2048]{1,0:T(8,128)(2,1)} %get-tuple-element.63), channel_id=1, source_target_pairs={{0,4},{1,5},{2,6},{3,7},{4,0},{5,1},{6,2},{7,3},{8,12},{9,13},{10,... | collective-permute-start | bytes 786440 | tf_op jit(solution)/shard_map/ppermute | solution.py:42
  30.3 15.5 %collective-permute-start.7 = (bf16[64,2048]{1,0:T(8,128)(2,1)}, bf16[64,2048]{1,0:T(8,128)(2,1)S(1)}, u32[]{:S(2)}, u32[]{:S(2)}) collective-permute-start(bf16[64,2048]{1,0:T(8,128)(2,1)} %get-tuple-element.63), channel_id=1, source_target_pairs={{0,8},{1,9},{2,10},{3,11},{4,12},{5,13},{6,14},{7,15},{8,0},{9,1},... | collective-permute-start | bytes 786440 | tf_op jit(solution)/shard_map/ppermute | solution.py:42
  38.5 47.4 %collective-permute-start.3 = (bf16[256,2048]{1,0:T(8,128)(2,1)S(1)}, bf16[256,2048]{1,0:T(8,128)(2,1)S(1)}, u32[]{:S(2)}, u32[]{:S(2)}) collective-permute-start(bf16[256,2048]{1,0:T(8,128)(2,1)S(1)} %pad_maximum_fusion.2), channel_id=1, source_target_pairs={{0,16},{1,17},{2,18},{3,19},{4,20},{5,21},{6,22},{7,23},{8,24},{9,... | collective-permute-start | bytes 3145736 | tf_op jit(solution)/shard_map/ppermute | solution.py:42
  42.4 31.8 %collective-permute-start.2 = (bf16[32,2048]{1,0:T(8,128)(2,1)S(1)}, bf16[32,2048]{1,0:T(8,128)(2,1)S(1)}, u32[]{:S(2)}, u32[]{:S(2)}) collective-permute-start(bf16[32,2048]{1,0:T(8,128)(2,1)S(1)} %pad_maximum_fusion.5), channel_id=1, source_target_pairs={{0,16},{1,17},{2,18},{3,19},{4,20},{5,21},{6,22},{7,23},{8,24},{9,... | collective-permute-start | bytes 393224 | tf_op jit(solution)/shard_map/ppermute | solution.py:42
  44.8 12.0 %collective-permute-start.15 = (bf16[2,128,512]{2,1,0:T(8,128)(2,1)S(1)}, bf16[2,128,512]{2,1,0:T(8,128)(2,1)S(1)}, u32[]{:S(2)}, u32[]{:S(2)}) collective-permute-start(bf16[2,128,512]{2,1,0:T(8,128)(2,1)S(1)} %maximum_select_fusion.8), channel_id=1, source_target_pairs={{0,1},{1,0},{2,3},{3,2},{4,5},{5,4},{6,7},{7,6},{8,9},{9,8},{10,11... | collective-permute-start | bytes 786440 | tf_op jit(solution)/shard_map/ppermute | solution.py:42
  45.8 10.9 %collective-permute-start.14 = (bf16[2,128,512]{2,1,0:T(8,128)(2,1)S(1)}, bf16[2,128,512]{2,1,0:T(8,128)(2,1)S(1)}, u32[]{:S(2)}, u32[]{:S(2)}) collective-permute-start(bf16[2,128,512]{2,1,0:T(8,128)(2,1)S(1)} %maximum_select_fusion.9), channel_id=1, source_target_pairs={{0,2},{1,3},{2,0},{3,1},{4,6},{5,7},{6,4},{7,5},{8,10},{9,11},{10,... | collective-permute-start | bytes 786440 | tf_op jit(solution)/shard_map/ppermute | solution.py:42
  56.8 12.3 %collective-permute-start.9 = (bf16[64,2048]{1,0:T(8,128)(2,1)S(1)}, bf16[64,2048]{1,0:T(8,128)(2,1)S(1)}, u32[]{:S(2)}, u32[]{:S(2)}) collective-permute-start(bf16[64,2048]{1,0:T(8,128)(2,1)S(1)} %collective-permute-done.7), channel_id=1, source_target_pairs={{0,4},{1,5},{2,6},{3,7},{4,0},{5,1},{6,2},{7,3},{8,12},{9,13},{10,... | collective-permute-start | bytes 786440 | tf_op jit(solution)/shard_map/ppermute | solution.py:42
  72.4 11.9 %collective-permute-start.21 = (bf16[128,512]{0,1:T(8,128)(2,1)S(1)}, bf16[128,512]{0,1:T(8,128)(2,1)S(1)}, u32[]{:S(2)}, u32[]{:S(2)}) collective-permute-start(bf16[128,512]{0,1:T(8,128)(2,1)S(1)} %get-tuple-element.55), channel_id=1, source_target_pairs={{0,8},{1,9},{2,10},{3,11},{4,12},{5,13},{6,14},{7,15},{8,0},{9,1},... | collective-permute-start | bytes 393224 | tf_op jit(solution)/shard_map/ppermute | solution.py:42
  99.1 24.0 %collective-permute-start.27 = (bf16[128,512]{1,0:T(8,128)(2,1)S(1)}, bf16[128,512]{1,0:T(8,128)(2,1)S(1)}, u32[]{:S(2)}, u32[]{:S(2)}) collective-permute-start(bf16[128,512]{1,0:T(8,128)(2,1)S(1)} %get-tuple-element.47), channel_id=1, source_target_pairs={{0,12},{1,13},{2,14},{3,15},{4,8},{5,9},{6,10},{7,11},{8,4},{9,5},... | collective-permute-start | bytes 393224 | tf_op jit(solution)/shard_map/ppermute | solution.py:42
  104.5 18.6 %collective-permute-start.28 = (bf16[128,512]{1,0:T(8,128)(2,1)S(1)}, bf16[128,512]{1,0:T(8,128)(2,1)S(1)}, u32[]{:S(2)}, u32[]{:S(2)}) collective-permute-start(bf16[128,512]{1,0:T(8,128)(2,1)S(1)} %get-tuple-element.46), channel_id=1, source_target_pairs={{0,8},{1,9},{2,10},{3,11},{4,12},{5,13},{6,14},{7,15},{8,0},{9,1},... | collective-permute-start | bytes 393224 | tf_op jit(solution)/shard_map/ppermute | solution.py:42
  104.5 15.5 %collective-permute-start.26 = (bf16[128,512]{1,0:T(8,128)(2,1)S(1)}, bf16[128,512]{1,0:T(8,128)(2,1)S(1)}, u32[]{:S(2)}, u32[]{:S(2)}) collective-permute-start(bf16[128,512]{1,0:T(8,128)(2,1)S(1)} %get-tuple-element.49), channel_id=1, source_target_pairs={{0,4},{1,5},{2,6},{3,7},{4,0},{5,1},{6,2},{7,3},{8,12},{9,13},{10,... | collective-permute-start | bytes 393224 | tf_op jit(solution)/shard_map/ppermute | solution.py:42
  113.8 27.0 %collective-permute-start.25 = (bf16[128,2048]{1,0:T(8,128)(2,1)S(1)}, bf16[128,2048]{1,0:T(8,128)(2,1)S(1)}, u32[]{:S(2)}, u32[]{:S(2)}) collective-permute-start(bf16[128,2048]{1,0:T(8,128)(2,1)S(1)} %get-tuple-element.12), channel_id=1, source_target_pairs={{16,0},{17,1},{18,2},{19,3},{20,4},{21,5},{22,6},{23,7},{24,8},{25... | collective-permute-start | bytes 1572872 | tf_op jit(solution)/shard_map/ppermute | solution.py:42
  115.1 25.6 %collective-permute-start.24 = (bf16[144,2048]{1,0:T(8,128)(2,1)S(1)}, bf16[144,2048]{1,0:T(8,128)(2,1)S(1)}, u32[]{:S(2)}, u32[]{:S(2)}) collective-permute-start(bf16[144,2048]{1,0:T(8,128)(2,1)S(1)} %pad_maximum_fusion.3), channel_id=1, source_target_pairs={{0,16},{1,17},{2,18},{3,19},{4,20},{5,21},{6,22},{7,23},{8,24},{9,... | collective-permute-start | bytes 1769480 | tf_op jit(solution)/shard_map/ppermute | solution.py:42
  123.1 10.8 %collective-permute-start.31 = (bf16[2,128,512]{2,1,0:T(8,128)(2,1)S(1)}, bf16[2,128,512]{2,1,0:T(8,128)(2,1)S(1)}, u32[]{:S(2)}, u32[]{:S(2)}) collective-permute-start(bf16[2,128,512]{2,1,0:T(8,128)(2,1)S(1)} %maximum_select_fusion.12), channel_id=1, source_target_pairs={{0,1},{1,0},{2,3},{3,2},{4,5},{5,4},{6,7},{7,6},{8,9},{9,8},{10,11... | collective-permute-start | bytes 786440 | tf_op jit(solution)/shard_map/ppermute | solution.py:42
  137.2 13.6 %collective-permute-start.35 = (bf16[128,512]{0,1:T(8,128)(2,1)S(1)}, bf16[128,512]{0,1:T(8,128)(2,1)S(1)}, u32[]{:S(2)}, u32[]{:S(2)}) collective-permute-start(bf16[128,512]{0,1:T(8,128)(2,1)S(1)} %get-tuple-element.41), channel_id=1, source_target_pairs={{0,4},{1,5},{2,6},{3,7},{4,0},{5,1},{6,2},{7,3},{8,12},{9,13},{10,... | collective-permute-start | bytes 393224 | tf_op jit(solution)/shard_map/ppermute | solution.py:42
  137.6 13.3 %collective-permute-start.36 = (bf16[128,512]{0,1:T(8,128)(2,1)S(1)}, bf16[128,512]{0,1:T(8,128)(2,1)S(1)}, u32[]{:S(2)}, u32[]{:S(2)}) collective-permute-start(bf16[128,512]{0,1:T(8,128)(2,1)S(1)} %get-tuple-element.43), channel_id=1, source_target_pairs={{0,12},{1,13},{2,14},{3,15},{4,8},{5,9},{6,10},{7,11},{8,4},{9,5},... | collective-permute-start | bytes 393224 | tf_op jit(solution)/shard_map/ppermute | solution.py:42
  139.4 13.1 %collective-permute-start.37 = (bf16[128,512]{0,1:T(8,128)(2,1)S(1)}, bf16[128,512]{0,1:T(8,128)(2,1)S(1)}, u32[]{:S(2)}, u32[]{:S(2)}) collective-permute-start(bf16[128,512]{0,1:T(8,128)(2,1)S(1)} %get-tuple-element.42), channel_id=1, source_target_pairs={{0,8},{1,9},{2,10},{3,11},{4,12},{5,13},{6,14},{7,15},{8,0},{9,1},... | collective-permute-start | bytes 393224 | tf_op jit(solution)/shard_map/ppermute | solution.py:42
  157.1 23.5 %collective-permute-start.43 = (bf16[128,512]{1,0:T(8,128)(2,1)S(1)}, bf16[128,512]{1,0:T(8,128)(2,1)S(1)}, u32[]{:S(2)}, u32[]{:S(2)}) collective-permute-start(bf16[128,512]{1,0:T(8,128)(2,1)S(1)} %get-tuple-element.34), channel_id=1, source_target_pairs={{0,12},{1,13},{2,14},{3,15},{4,8},{5,9},{6,10},{7,11},{8,4},{9,5},... | collective-permute-start | bytes 393224 | tf_op jit(solution)/shard_map/ppermute | solution.py:42
  163.0 17.7 %collective-permute-start.44 = (bf16[128,512]{1,0:T(8,128)(2,1)S(1)}, bf16[128,512]{1,0:T(8,128)(2,1)S(1)}, u32[]{:S(2)}, u32[]{:S(2)}) collective-permute-start(bf16[128,512]{1,0:T(8,128)(2,1)S(1)} %get-tuple-element.33), channel_id=1, source_target_pairs={{0,8},{1,9},{2,10},{3,11},{4,12},{5,13},{6,14},{7,15},{8,0},{9,1},... | collective-permute-start | bytes 393224 | tf_op jit(solution)/shard_map/ppermute | solution.py:42
  163.0 15.5 %collective-permute-start.42 = (bf16[128,512]{1,0:T(8,128)(2,1)S(1)}, bf16[128,512]{1,0:T(8,128)(2,1)S(1)}, u32[]{:S(2)}, u32[]{:S(2)}) collective-permute-start(bf16[128,512]{1,0:T(8,128)(2,1)S(1)} %get-tuple-element.36), channel_id=1, source_target_pairs={{0,4},{1,5},{2,6},{3,7},{4,0},{5,1},{6,2},{7,3},{8,12},{9,13},{10,... | collective-permute-start | bytes 393224 | tf_op jit(solution)/shard_map/ppermute | solution.py:42
  172.3 26.0 %collective-permute-start.41 = (bf16[128,2048]{1,0:T(8,128)(2,1)S(1)}, bf16[128,2048]{1,0:T(8,128)(2,1)S(1)}, u32[]{:S(2)}, u32[]{:S(2)}) collective-permute-start(bf16[128,2048]{1,0:T(8,128)(2,1)S(1)} %get-tuple-element.16), channel_id=1, source_target_pairs={{16,0},{17,1},{18,2},{19,3},{20,4},{21,5},{22,6},{23,7},{24,8},{25... | collective-permute-start | bytes 1572872 | tf_op jit(solution)/shard_map/ppermute | solution.py:42
  173.6 24.7 %collective-permute-start.40 = (bf16[144,2048]{1,0:T(8,128)(2,1)S(1)}, bf16[144,2048]{1,0:T(8,128)(2,1)S(1)}, u32[]{:S(2)}, u32[]{:S(2)}) collective-permute-start(bf16[144,2048]{1,0:T(8,128)(2,1)S(1)} %pad_maximum_fusion.4), channel_id=1, source_target_pairs={{0,16},{1,17},{2,18},{3,19},{4,20},{5,21},{6,22},{7,23},{8,24},{9,... | collective-permute-start | bytes 1769480 | tf_op jit(solution)/shard_map/ppermute | solution.py:42
  180.6 10.8 %collective-permute-start.47 = (bf16[2,128,512]{2,1,0:T(8,128)(2,1)S(1)}, bf16[2,128,512]{2,1,0:T(8,128)(2,1)S(1)}, u32[]{:S(2)}, u32[]{:S(2)}) collective-permute-start(bf16[2,128,512]{2,1,0:T(8,128)(2,1)S(1)} %maximum_select_fusion.16), channel_id=1, source_target_pairs={{0,1},{1,0},{2,3},{3,2},{4,5},{5,4},{6,7},{7,6},{8,9},{9,8},{10,11... | collective-permute-start | bytes 786440 | tf_op jit(solution)/shard_map/ppermute | solution.py:42
  194.8 14.5 %collective-permute-start.51 = (bf16[128,512]{0,1:T(8,128)(2,1)S(1)}, bf16[128,512]{0,1:T(8,128)(2,1)S(1)}, u32[]{:S(2)}, u32[]{:S(2)}) collective-permute-start(bf16[128,512]{0,1:T(8,128)(2,1)S(1)} %get-tuple-element.28), channel_id=1, source_target_pairs={{0,4},{1,5},{2,6},{3,7},{4,0},{5,1},{6,2},{7,3},{8,12},{9,13},{10,... | collective-permute-start | bytes 393224 | tf_op jit(solution)/shard_map/ppermute | solution.py:42
  195.4 13.9 %collective-permute-start.52 = (bf16[128,512]{0,1:T(8,128)(2,1)S(1)}, bf16[128,512]{0,1:T(8,128)(2,1)S(1)}, u32[]{:S(2)}, u32[]{:S(2)}) collective-permute-start(bf16[128,512]{0,1:T(8,128)(2,1)S(1)} %get-tuple-element.30), channel_id=1, source_target_pairs={{0,12},{1,13},{2,14},{3,15},{4,8},{5,9},{6,10},{7,11},{8,4},{9,5},... | collective-permute-start | bytes 393224 | tf_op jit(solution)/shard_map/ppermute | solution.py:42
  198.3 12.0 %collective-permute-start.53 = (bf16[128,512]{0,1:T(8,128)(2,1)S(1)}, bf16[128,512]{0,1:T(8,128)(2,1)S(1)}, u32[]{:S(2)}, u32[]{:S(2)}) collective-permute-start(bf16[128,512]{0,1:T(8,128)(2,1)S(1)} %get-tuple-element.29), channel_id=1, source_target_pairs={{0,8},{1,9},{2,10},{3,11},{4,12},{5,13},{6,14},{7,15},{8,0},{9,1},... | collective-permute-start | bytes 393224 | tf_op jit(solution)/shard_map/ppermute | solution.py:42
  (30 other events, 222.5 us)
where the time goes:
time: 214 us; the launch traced here: 213 us
  starting transfers between devices  78.5 us (37%)
  waiting for transfers between devices  62.5 us (29%)
  Pallas kernels  47 us (22%)
  local copies, waits for them, and re-layouts  8.27 us (4%)
  matrix products  7.74 us (4%)
  other arithmetic  7.16 us (3%)
    ppermute x54, starting transfers between devices, send(): return lax.ppermute(value, BOTH, pairs)  78.5 us
    ppermute x54, waiting for transfers between devices, send(): return lax.ppermute(value, BOTH, pairs)  62.5 us
    pallas_call x2, Pallas kernels, update(): pl.pallas_call(update_body, out_shape=[wide_f32, field_f32, field_f32, fi...  21 us
    pallas_call x2, Pallas kernels, adjoint(): pl.pallas_call(adjoint_body, out_shape=[wide_f32, field_bf16], in_specs=[...  17.3 us
    pallas_call x1, Pallas kernels, begin(): pl.pallas_call(begin_body, out_shape=field_f32, in_specs=[scalars] + [who...  8.75 us
  transfers between devices with their start and end apart: 54, of which 19 were waited for; matrix products, arithmetic and copies ran while one was open for 7% of the time, Pallas kernels for 18%

commit v1 on v0

--- a/solution.py
+++ b/solution.py
@@ -68,14 +68,23 @@
             bit *= 2
         return value
 
-    half = rows // 2
-    north_blocks = {0: (north_corr[:half], north_corr[half:])}
+    share = 2 if subs % 2 == 0 and rows % 32 == 0 else 1
+    half = rows // share
+    first = (sub % share) * half
+    gathered = {0: lax.dynamic_slice_in_dim(north_corr, first, half, axis=0)}
     bit = nz // 2
     while bit >= 1:
-        for j, parts in list(north_blocks.items()):
-            north_blocks[j ^ bit] = tuple(by_z(part, bit) for part in parts)
+        for j, part in list(gathered.items()):
+            gathered[j ^ bit] = by_z(part, bit)
         bit //= 2
-    north_rel = jnp.concatenate([part for j in range(nz) for part in north_blocks[j]], axis=0)
+    north_rel = lax.dynamic_update_slice(
+        jnp.zeros((nz * rows, strips * rows), jnp.bfloat16), north_corr, (0, 0)
+    )
+    for j in range(1, nz):
+        north_rel = lax.dynamic_update_slice(north_rel, gathered[j], (j * rows + first, 0))
+        if share == 2:
+            other = send(gathered[j], lambda s, t: (s ^ 1, t))
+            north_rel = lax.dynamic_update_slice(north_rel, other, (j * rows + half - first, 0))
 
     def cut(low):
         return [lax.dynamic_slice_in_dim(low, (my_z ^ j) * width, width, axis=1) for j in range(nz)]
@@ -128,48 +137,68 @@
     def rows_at(block):
         return pl.ds(pl.multiple_of(block * deep, deep), deep)
 
-    def laplace(source, block):
-        here = source[rows_at(block + 1), :]
+    lane = 128
+    chunk = 512 if cols % 512 == 0 else cols
+
+    def inner(at):
+        return pl.ds(lane + at, chunk)
+
+    def laplace(source, block, at):
+        wide = source[rows_at(block + 1), pl.ds(at, chunk + 2 * lane)]
+        here = wide[:, lane : lane + chunk]
         row = lax.broadcasted_iota(jnp.int32, here.shape, 0)
-        col = lax.broadcasted_iota(jnp.int32, here.shape, 1)
-        above = pltpu.roll(jnp.where(row == deep - 1, source[rows_at(block), :], here), 1, 0)
-        below = pltpu.roll(jnp.where(row == 0, source[rows_at(block + 2), :], here), deep - 1, 0)
-        left = jnp.where(col == 0, 0.0, pltpu.roll(here, 1, 1))
-        right = jnp.where(col == cols - 1, 0.0, pltpu.roll(here, cols - 1, 1))
-        return above + below + left + right - 4.0 * here
+        above = jnp.where(row == deep - 1, source[rows_at(block), inner(at)], here)
+        below = jnp.where(row == 0, source[rows_at(block + 2), inner(at)], here)
+        left = pltpu.roll(wide, 1, 1)[:, lane : lane + chunk]
+        right = pltpu.roll(wide, chunk + 2 * lane - 1, 1)[:, lane : lane + chunk]
+        return (
+            pltpu.roll(above, 1, 0) + pltpu.roll(below, deep - 1, 0) + left + right - 4.0 * here
+        )
+
+    together = max(n for n in (1, 2, 3) if blocks % n == 0)
+
+    def each_block(body):
+        def several(trip, carry):
+            for i in range(together):
+                for at in range(0, cols, chunk):
+                    body(trip * together + i, at)
+            return carry
+
+        lax.fori_loop(0, blocks // together, several, 0)
 
     def kept(ends_ref, block):
         return jnp.where(block == 0, ends_ref[0], jnp.where(block == blocks - 1, ends_ref[1], 1.0))
 
-    def clear_rims(buffer):
-        zero = jnp.zeros((deep, cols), f32)
-        for i in range(2):
-            buffer[i, :deep, :] = zero
-            buffer[i, tall_rows + deep :, :] = zero
-
-    def adjoint_body(ends_ref, mult, above, below, coef, pulled, middle, buffer):
-        clear_rims(buffer)
-        pulled[:deep, :] = above[...].astype(f32)
-        pulled[deep : rows + deep, :] = mult[...]
-        pulled[rows + deep :, :] = below[...].astype(f32)
-
-        def weigh(block, carry):
-            at = rows_at(block)
-            buffer[0, rows_at(block + 1), :] = coef[at, :] * pulled[at, :]
-            return carry
-
-        lax.fori_loop(0, blocks, weigh, 0)
+    padded = pltpu.VMEM((tall_rows + 2 * deep, cols + 2 * lane), f32)
+    inside = pl.ds(deep, tall_rows), pl.ds(lane, cols)
+
+    def clear_rims(*buffers):
+        high, broad = tall_rows + 2 * deep, cols + 2 * lane
+        for buffer in buffers:
+            buffer[:deep, :] = jnp.zeros((deep, broad), f32)
+            buffer[high - deep :, :] = jnp.zeros((deep, broad), f32)
+            buffer[:, :lane] = jnp.zeros((high, lane), f32)
+            buffer[:, broad - lane :] = jnp.zeros((high, lane), f32)
+
+    def adjoint_body(ends_ref, mult, above, below, coef, pulled, middle, one, two, first, second):
+        clear_rims(one, two)
+        first[:deep, :] = above[...].astype(f32)
+        first[deep : rows + deep, :] = mult[...]
+        first[rows + deep :, :] = below[...].astype(f32)
+        one[inside] = coef[...] * first[...]
         for step in range(STEPS):
-            source, target = buffer.at[step % 2], buffer.at[(step + 1) % 2]
-
-            def advance(block, carry):
-                at = rows_at(block)
-                value = (pulled[at, :] + laplace(source, block)) * kept(ends_ref, block)
-                pulled[at, :] = value
-                target[rows_at(block + 1), :] = coef[at, :] * value
-                return carry
-
-            lax.fori_loop(0, blocks, advance, 0)
+            source, target = (one, two) if step % 2 == 0 else (two, one)
+            now, later = (first, second) if step % 2 == 0 else (second, first)
+            later = pulled if step == STEPS - 1 else later
+
+            def advance(block, at):
+                spot = rows_at(block), pl.ds(at, chunk)
+                value = (now[spot] + laplace(source, block, at)) * kept(ends_ref, block)
+                later[spot] = value
+                if step < STEPS - 1:
+                    target[rows_at(block + 1), inner(at)] = coef[spot] * value
+
+            each_block(advance)
         middle[...] = pulled[deep : rows + deep, :].astype(bf16)
 
     def adjoint(multiplier, above, below):
@@ -178,55 +207,60 @@
             out_shape=[wide_f32, field_bf16],
             in_specs=[scalars] + [whole] * 4,
             out_specs=[whole] * 2,
-            scratch_shapes=[pltpu.VMEM((2, tall_rows + 2 * deep, cols), f32)],
+            scratch_shapes=[padded, padded] + [pltpu.VMEM((tall_rows, cols), f32)] * 2,
             compiler_params=limits,
             name="adjoint",
         )(ends, multiplier, above, below, diffuse_wide)
 
-    def propagate(ends_ref, coef, buffer):
+    def propagate(ends_ref, coef, one, two):
         for step in range(STEPS):
-            source, target = buffer.at[step % 2], buffer.at[(step + 1) % 2]
-
-            def advance(block, carry):
-                at = rows_at(block)
-                mid = rows_at(block + 1)
-                target[mid, :] = (
-                    source[mid, :] + coef[at, :] * laplace(source, block)
+            source, target = (one, two) if step % 2 == 0 else (two, one)
+
+            def advance(block, at):
+                mid = rows_at(block + 1), inner(at)
+                target[mid] = (
+                    source[mid]
+                    + coef[rows_at(block), pl.ds(at, chunk)] * laplace(source, block, at)
                 ) * kept(ends_ref, block)
-                return carry
-
-            lax.fori_loop(0, blocks, advance, 0)
-        return buffer[STEPS % 2, 2 * deep : rows + 2 * deep, :]
-
-    def begin_body(ends_ref, coef, past, forcing_ref, incr, target, buffer):
-        clear_rims(buffer)
-        buffer[0, deep : tall_rows + deep, :] = past[...]
-        target[...] = forcing_ref[...] - incr[...] + propagate(ends_ref, coef, buffer)
-
-    def begin(past, incr):
+
+            each_block(advance)
+        final = one if STEPS % 2 == 0 else two
+        return final[2 * deep : rows + 2 * deep, lane : lane + cols]
+
+    def begin_body(ends_ref, incr, own_coef, before, after, moved, one, two, coef):
+        clear_rims(one, two)
+        coef[:deep, :] = before[:deep, :].astype(f32)
+        coef[deep : rows + deep, :] = own_coef[...]
+        coef[rows + deep :, :] = after[:deep, :].astype(f32)
+        one[deep : 2 * deep, lane : lane + cols] = before[deep:, :].astype(f32)
+        one[2 * deep : rows + 2 * deep, lane : lane + cols] = incr[...]
+        one[rows + 2 * deep : rows + 3 * deep, lane : lane + cols] = after[deep:, :].astype(f32)
+        moved[...] = propagate(ends_ref, coef, one, two).astype(bf16)
+
+    def begin(incr, before, after):
         return pl.pallas_call(
             begin_body,
-            out_shape=field_f32,
+            out_shape=field_bf16,
             in_specs=[scalars] + [whole] * 4,
             out_specs=whole,
-            scratch_shapes=[pltpu.VMEM((2, tall_rows + 2 * deep, cols), f32)],
+            scratch_shapes=[padded, padded, pltpu.VMEM((tall_rows, cols), f32)],
             compiler_params=limits,
             name="begin",
-        )(ends, diffuse_wide, past, forcing, incr)
+        )(ends, incr, diffuse, before, after)
 
     def update_body(
         ends_ref, coef, past, arrived, pulled, mult, following, incr, forcing_ref,
-        past_new, incr_new, target, grad, buffer
+        past_new, incr_new, target, grad, one, two
     ):
-        clear_rims(buffer)
+        clear_rims(one, two)
         past_new[...] = past[...] + step_weight * (
             arrived[...].astype(f32) - ends_ref[2] * pulled[...]
         )
-        buffer[0, deep : tall_rows + deep, :] = past_new[...]
+        one[inside] = past_new[...]
         slope = mult[...] - following[...].astype(f32)
         grad[...] = slope
         incr_new[...] = incr[...] + step_weight * slope
-        target[...] = forcing_ref[...] - incr_new[...] + propagate(ends_ref, coef, buffer)
+        target[...] = forcing_ref[...] - incr_new[...] + propagate(ends_ref, coef, one, two)
 
     def update(past, arrived, pulled, mult, following, incr):
         return pl.pallas_call(
@@ -234,7 +268,7 @@
             out_shape=[wide_f32, field_f32, field_f32, field_f32],
             in_specs=[scalars] + [whole] * 8,
             out_specs=[whole] * 4,
-            scratch_shapes=[pltpu.VMEM((2, tall_rows + 2 * deep, cols), f32)],
+            scratch_shapes=[padded, padded],
             compiler_params=limits,
             name="update",
         )(ends, diffuse_wide, past, arrived, pulled, mult, following, incr, forcing)
@@ -246,6 +280,8 @@
     topmost = jnp.concatenate([short[:deep], short[rows : rows + deep]], axis=0)
     before = to_strip(lowest, 1)
     after = to_strip(topmost, -1)
+    moved = begin(incr_start[0], before, after)
+    arrived = to_sub(moved, 1).astype(f32)
     far = to_sub(short, 1).astype(f32)
     far_rims = to_sub(jnp.concatenate([before, after], axis=0), 1).astype(f32)
     diffuse_wide = jnp.concatenate(
@@ -273,7 +309,7 @@
     multiplier = mult_start[0]
     incr = incr_start[0]
     tile = product(spread(cut(multiplier.astype(jnp.bfloat16))))
-    target = begin(past_wide, incr)
+    target = forcing - incr + arrived
     for _ in range(ITERS):
         target, multiplier, incr, past_wide, tile, grad = advance(
             target, multiplier, incr, past_wide, tile

time: 214 us -> 218 us (1.019)
  waiting for transfers between devices: 62.5 us -> 84 us
  Pallas kernels: 47 us -> 32.6 us
  starting transfers between devices: 78.5 us -> 75.4 us
    ppermute x54 -> x55, waiting for transfers between devices: 62.5 us -> 84 us  [send(): return lax.ppermute(value, BOTH, pairs)]
    pallas_call x2, Pallas kernels: 17.3 us -> 11.5 us  [adjoint(): pl.pallas_call(adjoint_body, out_shape=[wide_f32, field_bf16], in_specs=[...]
    pallas_call x2, Pallas kernels: 21 us -> 15.4 us  [update(): pl.pallas_call(update_body, out_shape=[wide_f32, field_f32, field_f32, fi...]
    dynamic_update_slice x0 -> x7, local copies, waits for them, and re-layouts: none -> 4.62 us  [the longest x1 2.59 us: whole_step(): lax.dynamic_update_slice(jnp.zeros((nz * rows, strips * rows), jnp.bfloat...]
    unnamed x22 -> x18, local copies, waits for them, and re-layouts: 3.82 us -> 0.04 us
    ppermute x54 -> x55, starting transfers between devices: 78.5 us -> 75.4 us  [send(): return lax.ppermute(value, BOTH, pairs)]
    pallas_call x1, Pallas kernels: 8.75 us -> 5.7 us  [begin(): pl.pallas_call(begin_body, out_shape=field_bf16, in_specs=[scalars] + [wh...]
  transfers between devices with their start and end apart: 54 -> 55, of which waited for: 19 -> 21; matrix products, arithmetic and copies ran while one was open for 7% -> 8% of each run, Pallas kernels for 18% -> 15%
where the time goes in v1:
time: 218 us; the launch traced here: 217 us
  waiting for transfers between devices  84 us (39%)
  starting transfers between devices  75.4 us (35%)
  Pallas kernels  32.6 us (15%)
  local copies, waits for them, and re-layouts  9.02 us (4%)
  matrix products  7.88 us (4%)
  other arithmetic  6.78 us (3%)
    ppermute x55, waiting for transfers between devices, send(): return lax.ppermute(value, BOTH, pairs)  84 us
    ppermute x55, starting transfers between devices, send(): return lax.ppermute(value, BOTH, pairs)  75.4 us
    pallas_call x2, Pallas kernels, update(): pl.pallas_call(update_body, out_shape=[wide_f32, field_f32, field_f32, fi...  15.4 us
    pallas_call x2, Pallas kernels, adjoint(): pl.pallas_call(adjoint_body, out_shape=[wide_f32, field_bf16], in_specs=[...  11.5 us
    pallas_call x1, Pallas kernels, begin(): pl.pallas_call(begin_body, out_shape=field_bf16, in_specs=[scalars] + [wh...  5.7 us
  transfers between devices with their start and end apart: 55, of which 21 were waited for; matrix products, arithmetic and copies ran while one was open for 8% of the time, Pallas kernels for 15%

profile of v1, /device:TPU:0, one launch (start us, length us, event | category | flops | bytes accessed | tf_op | source)
XLA Modules:
  0.0 217.4 jit_solution(4423595577037780855)
XLA Ops:
  2.4 3.1 %collective-permute-start.5 = (bf16[64,2048]{1,0:T(8,128)(2,1)}, bf16[64,2048]{1,0:T(8,128)(2,1)}, u32[]{:S(2)}, u32[]{:S(2)}) collective-permute-start(bf16[64,2048]{1,0:T(8,128)(2,1)} %constant_dynamic-slice_fusion.9), channel_id=1, source_target_pairs={{0,4},{1,5},{2,6},{3,7},{4,0},{5,1},{6,2},{7,3},{8,12},{9,13},{10,... | collective-permute-start | bytes 786440 | tf_op jit(solution)/shard_map/ppermute | solution.py:42
  5.5 2.6 %collective-permute-start.7 = (bf16[64,2048]{1,0:T(8,128)(2,1)}, bf16[64,2048]{1,0:T(8,128)(2,1)}, u32[]{:S(2)}, u32[]{:S(2)}) collective-permute-start(bf16[64,2048]{1,0:T(8,128)(2,1)} %constant_dynamic-slice_fusion.9), channel_id=1, source_target_pairs={{0,8},{1,9},{2,10},{3,11},{4,12},{5,13},{6,14},{7,15},{8,0},{9,1},... | collective-permute-start | bytes 786440 | tf_op jit(solution)/shard_map/ppermute | solution.py:42
  15.9 2.6 %dynamic_update_slice.93 = bf16[512,2048]{1,0:T(8,128)(2,1)} pad(bf16[128,2048]{1,0:T(8,128)(2,1)} %param.10, bf16[]{:T(256)} %constant.206.clone.1), padding=0_384x0_0 | pad | bytes 2621442 | tf_op jit(solution)/shard_map/dynamic_update_slice | solution.py:80
  18.6 4.1 %collective-permute-start.13 = (bf16[128,512]{1,0:T(8,128)(2,1)}, bf16[128,512]{1,0:T(8,128)(2,1)S(1)}, u32[]{:S(2)}, u32[]{:S(2)}) collective-permute-start(bf16[128,512]{1,0:T(8,128)(2,1)} %get-tuple-element.59), channel_id=1, source_target_pairs={{0,8},{1,9},{2,10},{3,11},{4,12},{5,13},{6,14},{7,15},{8,0},{9,1},... | collective-permute-start | bytes 393224 | tf_op jit(solution)/shard_map/ppermute | solution.py:42
  22.7 3.7 %collective-permute-start.12 = (bf16[128,512]{1,0:T(8,128)(2,1)}, bf16[128,512]{1,0:T(8,128)(2,1)S(1)}, u32[]{:S(2)}, u32[]{:S(2)}) collective-permute-start(bf16[128,512]{1,0:T(8,128)(2,1)} %get-tuple-element.60), channel_id=1, source_target_pairs={{0,12},{1,13},{2,14},{3,15},{4,8},{5,9},{6,10},{7,11},{8,4},{9,5},... | collective-permute-start | bytes 393224 | tf_op jit(solution)/shard_map/ppermute | solution.py:42
  26.4 5.7 %begin.1 = bf16[128,2048]{1,0:T(8,128)(2,1)S(1)} custom-call(f32[3]{0:T(128)S(1)} %add_convert_fusion.ends_ref, f32[128,2048]{1,0:T(8,128)S(1)} %bitcast.160, f32[128,2048]{1,0:T(8,128)S(1)} %bitcast.164, bf16[16,2048]{1,0:T(8,128)(2,1)S(1)} %collective-permute-done.before, bf16[16,2048]{1,0:T(8,128)(2,1)S(1)} %collective-permute-done.1.after), custom_call_target="tpu_custom_call" | custom-call | tf_op jit(solution)/shard_map/begin/pallas_call | solution.py:241
  32.1 3.5 %collective-permute-start.3 = (bf16[256,2048]{1,0:T(8,128)(2,1)S(1)}, bf16[256,2048]{1,0:T(8,128)(2,1)S(1)}, u32[]{:S(2)}, u32[]{:S(2)}) collective-permute-start(bf16[256,2048]{1,0:T(8,128)(2,1)S(1)} %copy-done.5), channel_id=1, source_target_pairs={{0,16},{1,17},{2,18},{3,19},{4,20},{5,21},{6,22},{7,23},{8,24},{9,... | collective-permute-start | bytes 3145736 | tf_op jit(solution)/shard_map/ppermute | solution.py:42
  40.6 5.7 %collective-permute-done.14 = bf16[2,128,512]{2,1,0:T(8,128)(2,1)S(1)} collective-permute-done((bf16[2,128,512]{2,1,0:T(8,128)(2,1)S(1)}, bf16[2,128,512]{2,1,0:T(8,128)(2,1)S(1)}, u32[]{:S(2)}, u32[]{:S(2)}) %collective-permute-start.14) | collective-permute-done | bytes 262176 | tf_op jit(solution)/shard_map/ppermute | solution.py:42
  46.4 4.0 %collective-permute-done.15 = bf16[2,128,512]{2,1,0:T(8,128)(2,1)S(1)} collective-permute-done((bf16[2,128,512]{2,1,0:T(8,128)(2,1)S(1)}, bf16[2,128,512]{2,1,0:T(8,128)(2,1)S(1)}, u32[]{:S(2)}, u32[]{:S(2)}) %collective-permute-start.15) | collective-permute-done | bytes 262176 | tf_op jit(solution)/shard_map/ppermute | solution.py:42
  50.6 3.9 %collective-permute-start.2 = (bf16[32,2048]{1,0:T(8,128)(2,1)S(1)}, bf16[32,2048]{1,0:T(8,128)(2,1)S(1)}, u32[]{:S(2)}, u32[]{:S(2)}) collective-permute-start(bf16[32,2048]{1,0:T(8,128)(2,1)S(1)} %pad_maximum_fusion.5), channel_id=1, source_target_pairs={{0,16},{1,17},{2,18},{3,19},{4,20},{5,21},{6,22},{7,23},{8,24},{9,... | collective-permute-start | bytes 393224 | tf_op jit(solution)/shard_map/ppermute | solution.py:42
  54.7 21.4 %collective-permute-done.6 = bf16[64,2048]{1,0:T(8,128)(2,1)S(1)} collective-permute-done((bf16[64,2048]{1,0:T(8,128)(2,1)}, bf16[64,2048]{1,0:T(8,128)(2,1)S(1)}, u32[]{:S(2)}, u32[]{:S(2)}) %collective-permute-start.6) | collective-permute-done | bytes 262176 | tf_op jit(solution)/shard_map/ppermute | solution.py:42
  77.0 4.9 %collective-permute-done.8 = bf16[64,2048]{1,0:T(8,128)(2,1)S(1)} collective-permute-done((bf16[64,2048]{1,0:T(8,128)(2,1)}, bf16[64,2048]{1,0:T(8,128)(2,1)S(1)}, u32[]{:S(2)}, u32[]{:S(2)}) %collective-permute-start.8) | collective-permute-done | bytes 262176 | tf_op jit(solution)/shard_map/ppermute | solution.py:42
  85.9 6.5 %collective-permute-done.10 = bf16[64,2048]{1,0:T(8,128)(2,1)S(1)} collective-permute-done((bf16[64,2048]{1,0:T(8,128)(2,1)S(1)}, bf16[64,2048]{1,0:T(8,128)(2,1)S(1)}, u32[]{:S(2)}, u32[]{:S(2)}) %collective-permute-start.10) | collective-permute-done | bytes 262176 | tf_op jit(solution)/shard_map/ppermute | solution.py:42
  97.5 2.4 %collective-permute-done.20 = bf16[128,512]{0,1:T(8,128)(2,1)S(1)} collective-permute-done((bf16[128,512]{0,1:T(8,128)(2,1)S(1)}, bf16[128,512]{0,1:T(8,128)(2,1)S(1)}, u32[]{:S(2)}, u32[]{:S(2)}) %collective-permute-start.20) | collective-permute-done | bytes 131104 | tf_op jit(solution)/shard_map/ppermute | solution.py:42
  99.9 3.5 %collective-permute-done.21 = bf16[128,512]{0,1:T(8,128)(2,1)S(1)} collective-permute-done((bf16[128,512]{0,1:T(8,128)(2,1)S(1)}, bf16[128,512]{0,1:T(8,128)(2,1)S(1)}, u32[]{:S(2)}, u32[]{:S(2)}) %collective-permute-start.21) | collective-permute-done | bytes 131104 | tf_op jit(solution)/shard_map/ppermute | solution.py:42
  103.3 5.2 %collective-permute-done.22 = bf16[128,512]{0,1:T(8,128)(2,1)S(1)} collective-permute-done((bf16[128,512]{0,1:T(8,128)(2,1)S(1)}, bf16[128,512]{0,1:T(8,128)(2,1)S(1)}, u32[]{:S(2)}, u32[]{:S(2)}) %collective-permute-start.22) | collective-permute-done | bytes 131104 | tf_op jit(solution)/shard_map/ppermute | solution.py:42
  113.0 5.1 %collective-permute-start.28 = (bf16[128,512]{1,0:T(8,128)(2,1)S(1)}, bf16[128,512]{1,0:T(8,128)(2,1)S(1)}, u32[]{:S(2)}, u32[]{:S(2)}) collective-permute-start(bf16[128,512]{1,0:T(8,128)(2,1)S(1)} %get-tuple-element.47), channel_id=1, source_target_pairs={{0,12},{1,13},{2,14},{3,15},{4,8},{5,9},{6,10},{7,11},{8,4},{9,5},... | collective-permute-start | bytes 393224 | tf_op jit(solution)/shard_map/ppermute | solution.py:42
  118.9 3.7 %collective-permute-start.25 = (bf16[144,2048]{1,0:T(8,128)(2,1)S(1)}, bf16[144,2048]{1,0:T(8,128)(2,1)S(1)}, u32[]{:S(2)}, u32[]{:S(2)}) collective-permute-start(bf16[144,2048]{1,0:T(8,128)(2,1)S(1)} %pad_maximum_fusion.3), channel_id=1, source_target_pairs={{0,16},{1,17},{2,18},{3,19},{4,20},{5,21},{6,22},{7,23},{8,24},{9,... | collective-permute-start | bytes 1769480 | tf_op jit(solution)/shard_map/ppermute | solution.py:42
  122.5 3.2 %collective-permute-done.27 = bf16[128,512]{1,0:T(8,128)(2,1)S(1)} collective-permute-done((bf16[128,512]{1,0:T(8,128)(2,1)S(1)}, bf16[128,512]{1,0:T(8,128)(2,1)S(1)}, u32[]{:S(2)}, u32[]{:S(2)}) %collective-permute-start.27) | collective-permute-done | bytes 131104 | tf_op jit(solution)/shard_map/ppermute | solution.py:42
  126.3 2.7 %collective-permute-done.29 = bf16[128,512]{1,0:T(8,128)(2,1)S(1)} collective-permute-done((bf16[128,512]{1,0:T(8,128)(2,1)S(1)}, bf16[128,512]{1,0:T(8,128)(2,1)S(1)}, u32[]{:S(2)}, u32[]{:S(2)}) %collective-permute-start.29) | collective-permute-done | bytes 131104 | tf_op jit(solution)/shard_map/ppermute | solution.py:42
  130.6 5.8 %adjoint.2 = (f32[144,2048]{1,0:T(8,128)S(1)}, bf16[128,2048]{1,0:T(8,128)(2,1)S(1)}) custom-call(f32[3]{0:T(128)S(1)} %add_convert_fusion.ends_ref, f32[128,2048]{1,0:T(8,128)S(1)} %get-tuple-element.23.mult, bf16[8,2048]{1,0:T(8,128)(2,1)S(1)} %collective-permute-done.23.above, bf16[8,2048]{1,0:T(8,128)(2,1)S(1)} %collective-permute-done.24.below, ...), custom_call_target="tpu_custom_call" | custom-call | tf_op jit(solution)/shard_map/adjoint/pallas_call | solution.py:205
  143.8 3.0 %collective-permute-start.37 = (bf16[128,512]{0,1:T(8,128)(2,1)S(1)}, bf16[128,512]{0,1:T(8,128)(2,1)S(1)}, u32[]{:S(2)}, u32[]{:S(2)}) collective-permute-start(bf16[128,512]{0,1:T(8,128)(2,1)S(1)} %get-tuple-element.43), channel_id=1, source_target_pairs={{0,12},{1,13},{2,14},{3,15},{4,8},{5,9},{6,10},{7,11},{8,4},{9,5},... | collective-permute-start | bytes 393224 | tf_op jit(solution)/shard_map/ppermute | solution.py:42
  146.9 5.7 %collective-permute-done.26.following = bf16[128,2048]{1,0:T(8,128)(2,1)S(1)} collective-permute-done((bf16[128,2048]{1,0:T(8,128)(2,1)S(1)}, bf16[128,2048]{1,0:T(8,128)(2,1)S(1)}, u32[]{:S(2)}, u32[]{:S(2)}) %collective-permute-start.26) | collective-permute-done | bytes 524320 | tf_op jit(solution)/shard_map/ppermute | solution.py:42
  152.6 7.3 %update.2 = (f32[144,2048]{1,0:T(8,128)S(1)}, f32[128,2048]{1,0:T(8,128)S(1)}, f32[128,2048]{1,0:T(8,128)S(1)}, f32[128,2048]{1,0:T(8,128)}) custom-call(f32[3]{0:T(128)S(1)} %add_convert_fusion.ends_ref, f32[144,2048]{1,0:T(8,128)S(1)} %pad_maximum_fusion.coef, f32[144,2048]{1,0:T(8,128)S(1)} %pad_maximum_fusion.1.past, ...), custom_call_target="tpu_custom_call" | custom-call | tf_op jit(solution)/shard_map/update/pallas_call | solution.py:266
  164.7 5.5 %collective-permute-start.44 = (bf16[128,512]{1,0:T(8,128)(2,1)S(1)}, bf16[128,512]{1,0:T(8,128)(2,1)S(1)}, u32[]{:S(2)}, u32[]{:S(2)}) collective-permute-start(bf16[128,512]{1,0:T(8,128)(2,1)S(1)} %get-tuple-element.34), channel_id=1, source_target_pairs={{0,12},{1,13},{2,14},{3,15},{4,8},{5,9},{6,10},{7,11},{8,4},{9,5},... | collective-permute-start | bytes 393224 | tf_op jit(solution)/shard_map/ppermute | solution.py:42
  170.9 5.8 %adjoint.3 = (f32[144,2048]{1,0:T(8,128)S(1)}, bf16[128,2048]{1,0:T(8,128)(2,1)S(1)}) custom-call(f32[3]{0:T(128)S(1)} %add_convert_fusion.ends_ref, f32[128,2048]{1,0:T(8,128)S(1)} %get-tuple-element.21.mult, bf16[8,2048]{1,0:T(8,128)(2,1)S(1)} %collective-permute-done.39.above, bf16[8,2048]{1,0:T(8,128)(2,1)S(1)} %collective-permute-done.40.below, ...), custom_call_target="tpu_custom_call" | custom-call | tf_op jit(solution)/shard_map/adjoint/pallas_call | solution.py:205
  178.0 4.8 %collective-permute-start.41 = (bf16[144,2048]{1,0:T(8,128)(2,1)S(1)}, bf16[144,2048]{1,0:T(8,128)(2,1)S(1)}, u32[]{:S(2)}, u32[]{:S(2)}) collective-permute-start(bf16[144,2048]{1,0:T(8,128)(2,1)S(1)} %pad_maximum_fusion.4), channel_id=1, source_target_pairs={{0,16},{1,17},{2,18},{3,19},{4,20},{5,21},{6,22},{7,23},{8,24},{9,... | collective-permute-start | bytes 1769480 | tf_op jit(solution)/shard_map/ppermute | solution.py:42
  185.7 6.6 %collective-permute-done.46 = bf16[2,128,512]{2,1,0:T(8,128)(2,1)S(1)} collective-permute-done((bf16[2,128,512]{2,1,0:T(8,128)(2,1)S(1)}, bf16[2,128,512]{2,1,0:T(8,128)(2,1)S(1)}, u32[]{:S(2)}, u32[]{:S(2)}) %collective-permute-start.46) | collective-permute-done | bytes 262176 | tf_op jit(solution)/shard_map/ppermute | solution.py:42
  192.4 3.6 %collective-permute-done.47 = bf16[2,128,512]{2,1,0:T(8,128)(2,1)S(1)} collective-permute-done((bf16[2,128,512]{2,1,0:T(8,128)(2,1)S(1)}, bf16[2,128,512]{2,1,0:T(8,128)(2,1)S(1)}, u32[]{:S(2)}, u32[]{:S(2)}) %collective-permute-start.47) | collective-permute-done | bytes 262176 | tf_op jit(solution)/shard_map/ppermute | solution.py:42
  200.0 2.6 %collective-permute-start.53 = (bf16[128,512]{0,1:T(8,128)(2,1)S(1)}, bf16[128,512]{0,1:T(8,128)(2,1)S(1)}, u32[]{:S(2)}, u32[]{:S(2)}) collective-permute-start(bf16[128,512]{0,1:T(8,128)(2,1)S(1)} %get-tuple-element.30), channel_id=1, source_target_pairs={{0,12},{1,13},{2,14},{3,15},{4,8},{5,9},{6,10},{7,11},{8,4},{9,5},... | collective-permute-start | bytes 393224 | tf_op jit(solution)/shard_map/ppermute | solution.py:42
  202.9 8.1 %update.3 = (f32[144,2048]{1,0:T(8,128)}, f32[128,2048]{1,0:T(8,128)}, f32[128,2048]{1,0:T(8,128)S(1)}, f32[128,2048]{1,0:T(8,128)}) custom-call(f32[3]{0:T(128)S(1)} %add_convert_fusion.ends_ref, f32[144,2048]{1,0:T(8,128)S(1)} %pad_maximum_fusion.coef, f32[144,2048]{1,0:T(8,128)S(1)} %get-tuple-element.13.past, ...), custom_call_target="tpu_custom_call" | custom-call | tf_op jit(solution)/shard_map/update/pallas_call | solution.py:266
  211.0 3.7 %collective-permute-done.54 = bf16[128,512]{0,1:T(8,128)(2,1)S(1)} collective-permute-done((bf16[128,512]{0,1:T(8,128)(2,1)S(1)}, bf16[128,512]{0,1:T(8,128)(2,1)S(1)}, u32[]{:S(2)}, u32[]{:S(2)}) %collective-permute-start.54) | collective-permute-done | bytes 131104 | tf_op jit(solution)/shard_map/ppermute | solution.py:42
  (183 shorter events, 55.7 us)
Async XLA Ops:
  2.4 36.5 %collective-permute-start.5 = (bf16[64,2048]{1,0:T(8,128)(2,1)}, bf16[64,2048]{1,0:T(8,128)(2,1)}, u32[]{:S(2)}, u32[]{:S(2)}) collective-permute-start(bf16[64,2048]{1,0:T(8,128)(2,1)} %constant_dynamic-slice_fusion.9), channel_id=1, source_target_pairs={{0,4},{1,5},{2,6},{3,7},{4,0},{5,1},{6,2},{7,3},{8,12},{9,13},{10,... | collective-permute-start | bytes 786440 | tf_op jit(solution)/shard_map/ppermute | solution.py:42
  5.5 45.1 %collective-permute-start.7 = (bf16[64,2048]{1,0:T(8,128)(2,1)}, bf16[64,2048]{1,0:T(8,128)(2,1)}, u32[]{:S(2)}, u32[]{:S(2)}) collective-permute-start(bf16[64,2048]{1,0:T(8,128)(2,1)} %constant_dynamic-slice_fusion.9), channel_id=1, source_target_pairs={{0,8},{1,9},{2,10},{3,11},{4,12},{5,13},{6,14},{7,15},{8,0},{9,1},... | collective-permute-start | bytes 786440 | tf_op jit(solution)/shard_map/ppermute | solution.py:42
  10.3 21.8 %collective-permute-start.11 = (bf16[128,512]{1,0:T(8,128)(2,1)}, bf16[128,512]{1,0:T(8,128)(2,1)S(1)}, u32[]{:S(2)}, u32[]{:S(2)}) collective-permute-start(bf16[128,512]{1,0:T(8,128)(2,1)} %get-tuple-element.62), channel_id=1, source_target_pairs={{0,4},{1,5},{2,6},{3,7},{4,0},{5,1},{6,2},{7,3},{8,12},{9,13},{10,... | collective-permute-start | bytes 393224 | tf_op jit(solution)/shard_map/ppermute | solution.py:42
  18.6 17.1 %collective-permute-start.13 = (bf16[128,512]{1,0:T(8,128)(2,1)}, bf16[128,512]{1,0:T(8,128)(2,1)S(1)}, u32[]{:S(2)}, u32[]{:S(2)}) collective-permute-start(bf16[128,512]{1,0:T(8,128)(2,1)} %get-tuple-element.59), channel_id=1, source_target_pairs={{0,8},{1,9},{2,10},{3,11},{4,12},{5,13},{6,14},{7,15},{8,0},{9,1},... | collective-permute-start | bytes 393224 | tf_op jit(solution)/shard_map/ppermute | solution.py:42
  22.7 14.4 %collective-permute-start.12 = (bf16[128,512]{1,0:T(8,128)(2,1)}, bf16[128,512]{1,0:T(8,128)(2,1)S(1)}, u32[]{:S(2)}, u32[]{:S(2)}) collective-permute-start(bf16[128,512]{1,0:T(8,128)(2,1)} %get-tuple-element.60), channel_id=1, source_target_pairs={{0,12},{1,13},{2,14},{3,15},{4,8},{5,9},{6,10},{7,11},{8,4},{9,5},... | collective-permute-start | bytes 393224 | tf_op jit(solution)/shard_map/ppermute | solution.py:42
  32.1 98.1 %collective-permute-start.3 = (bf16[256,2048]{1,0:T(8,128)(2,1)S(1)}, bf16[256,2048]{1,0:T(8,128)(2,1)S(1)}, u32[]{:S(2)}, u32[]{:S(2)}) collective-permute-start(bf16[256,2048]{1,0:T(8,128)(2,1)S(1)} %copy-done.5), channel_id=1, source_target_pairs={{0,16},{1,17},{2,18},{3,19},{4,20},{5,21},{6,22},{7,23},{8,24},{9,... | collective-permute-start | bytes 3145736 | tf_op jit(solution)/shard_map/ppermute | solution.py:42
  35.7 73.2 %collective-permute-start.4 = (bf16[128,2048]{1,0:T(8,128)(2,1)S(1)}, bf16[128,2048]{1,0:T(8,128)(2,1)S(1)}, u32[]{:S(2)}, u32[]{:S(2)}) collective-permute-start(bf16[128,2048]{1,0:T(8,128)(2,1)S(1)} %begin.1), channel_id=1, source_target_pairs={{0,16},{1,17},{2,18},{3,19},{4,20},{5,21},{6,22},{7,23},{8,24},{9,... | collective-permute-start | bytes 1572872 | tf_op jit(solution)/shard_map/ppermute | solution.py:42
  38.9 11.5 %collective-permute-start.15 = (bf16[2,128,512]{2,1,0:T(8,128)(2,1)S(1)}, bf16[2,128,512]{2,1,0:T(8,128)(2,1)S(1)}, u32[]{:S(2)}, u32[]{:S(2)}) collective-permute-start(bf16[2,128,512]{2,1,0:T(8,128)(2,1)S(1)} %maximum_select_fusion.9), channel_id=1, source_target_pairs={{0,2},{1,3},{2,0},{3,1},{4,6},{5,7},{6,4},{7,5},{8,10},{9,11},{10,... | collective-permute-start | bytes 786440 | tf_op jit(solution)/shard_map/ppermute | solution.py:42
  50.5 25.5 %collective-permute-start.6 = (bf16[64,2048]{1,0:T(8,128)(2,1)}, bf16[64,2048]{1,0:T(8,128)(2,1)S(1)}, u32[]{:S(2)}, u32[]{:S(2)}) collective-permute-start(bf16[64,2048]{1,0:T(8,128)(2,1)} %collective-permute-done.5), channel_id=1, source_target_pairs={{0,16},{1,17},{2,18},{3,19},{4,20},{5,21},{6,22},{7,23},{8,24},{9,... | collective-permute-start | bytes 786440 | tf_op jit(solution)/shard_map/ppermute | solution.py:42
  50.6 45.5 %collective-permute-start.2 = (bf16[32,2048]{1,0:T(8,128)(2,1)S(1)}, bf16[32,2048]{1,0:T(8,128)(2,1)S(1)}, u32[]{:S(2)}, u32[]{:S(2)}) collective-permute-start(bf16[32,2048]{1,0:T(8,128)(2,1)S(1)} %pad_maximum_fusion.5), channel_id=1, source_target_pairs={{0,16},{1,17},{2,18},{3,19},{4,20},{5,21},{6,22},{7,23},{8,24},{9,... | collective-permute-start | bytes 393224 | tf_op jit(solution)/shard_map/ppermute | solution.py:42
  54.5 27.4 %collective-permute-start.8 = (bf16[64,2048]{1,0:T(8,128)(2,1)}, bf16[64,2048]{1,0:T(8,128)(2,1)S(1)}, u32[]{:S(2)}, u32[]{:S(2)}) collective-permute-start(bf16[64,2048]{1,0:T(8,128)(2,1)} %collective-permute-done.7), channel_id=1, source_target_pairs={{0,16},{1,17},{2,18},{3,19},{4,20},{5,21},{6,22},{7,23},{8,24},{9,... | collective-permute-start | bytes 786440 | tf_op jit(solution)/shard_map/ppermute | solution.py:42
  96.1 12.4 %collective-permute-start.22 = (bf16[128,512]{0,1:T(8,128)(2,1)S(1)}, bf16[128,512]{0,1:T(8,128)(2,1)S(1)}, u32[]{:S(2)}, u32[]{:S(2)}) collective-permute-start(bf16[128,512]{0,1:T(8,128)(2,1)S(1)} %get-tuple-element.55), channel_id=1, source_target_pairs={{0,8},{1,9},{2,10},{3,11},{4,12},{5,13},{6,14},{7,15},{8,0},{9,1},... | collective-permute-start | bytes 393224 | tf_op jit(solution)/shard_map/ppermute | solution.py:42
  113.0 13.2 %collective-permute-start.28 = (bf16[128,512]{1,0:T(8,128)(2,1)S(1)}, bf16[128,512]{1,0:T(8,128)(2,1)S(1)}, u32[]{:S(2)}, u32[]{:S(2)}) collective-permute-start(bf16[128,512]{1,0:T(8,128)(2,1)S(1)} %get-tuple-element.47), channel_id=1, source_target_pairs={{0,12},{1,13},{2,14},{3,15},{4,8},{5,9},{6,10},{7,11},{8,4},{9,5},... | collective-permute-start | bytes 393224 | tf_op jit(solution)/shard_map/ppermute | solution.py:42
  118.2 10.8 %collective-permute-start.29 = (bf16[128,512]{1,0:T(8,128)(2,1)S(1)}, bf16[128,512]{1,0:T(8,128)(2,1)S(1)}, u32[]{:S(2)}, u32[]{:S(2)}) collective-permute-start(bf16[128,512]{1,0:T(8,128)(2,1)S(1)} %get-tuple-element.46), channel_id=1, source_target_pairs={{0,8},{1,9},{2,10},{3,11},{4,12},{5,13},{6,14},{7,15},{8,0},{9,1},... | collective-permute-start | bytes 393224 | tf_op jit(solution)/shard_map/ppermute | solution.py:42
  118.9 28.1 %collective-permute-start.25 = (bf16[144,2048]{1,0:T(8,128)(2,1)S(1)}, bf16[144,2048]{1,0:T(8,128)(2,1)S(1)}, u32[]{:S(2)}, u32[]{:S(2)}) collective-permute-start(bf16[144,2048]{1,0:T(8,128)(2,1)S(1)} %pad_maximum_fusion.3), channel_id=1, source_target_pairs={{0,16},{1,17},{2,18},{3,19},{4,20},{5,21},{6,22},{7,23},{8,24},{9,... | collective-permute-start | bytes 1769480 | tf_op jit(solution)/shard_map/ppermute | solution.py:42
  125.8 10.6 %collective-permute-start.30 = (bf16[2,128,512]{2,1,0:T(8,128)(2,1)S(1)}, bf16[2,128,512]{2,1,0:T(8,128)(2,1)S(1)}, u32[]{:S(2)}, u32[]{:S(2)}) collective-permute-start(bf16[2,128,512]{2,1,0:T(8,128)(2,1)S(1)} %maximum_select_fusion.12), channel_id=1, source_target_pairs={{0,2},{1,3},{2,0},{3,1},{4,6},{5,7},{6,4},{7,5},{8,10},{9,11},{10,... | collective-permute-start | bytes 786440 | tf_op jit(solution)/shard_map/ppermute | solution.py:42
  126.3 12.6 %collective-permute-start.32 = (bf16[2,128,512]{2,1,0:T(8,128)(2,1)S(1)}, bf16[2,128,512]{2,1,0:T(8,128)(2,1)S(1)}, u32[]{:S(2)}, u32[]{:S(2)}) collective-permute-start(bf16[2,128,512]{2,1,0:T(8,128)(2,1)S(1)} %maximum_select_fusion.12), channel_id=1, source_target_pairs={{0,1},{1,0},{2,3},{3,2},{4,5},{5,4},{6,7},{7,6},{8,9},{9,8},{10,11... | collective-permute-start | bytes 786440 | tf_op jit(solution)/shard_map/ppermute | solution.py:42
  129.0 9.8 %collective-permute-start.31 = (bf16[2,128,512]{2,1,0:T(8,128)(2,1)S(1)}, bf16[2,128,512]{2,1,0:T(8,128)(2,1)S(1)}, u32[]{:S(2)}, u32[]{:S(2)}) collective-permute-start(bf16[2,128,512]{2,1,0:T(8,128)(2,1)S(1)} %maximum_select_fusion.13), channel_id=1, source_target_pairs={{0,2},{1,3},{2,0},{3,1},{4,6},{5,7},{6,4},{7,5},{8,10},{9,11},{10,... | collective-permute-start | bytes 786440 | tf_op jit(solution)/shard_map/ppermute | solution.py:42
  136.4 16.2 %collective-permute-start.26 = (bf16[128,2048]{1,0:T(8,128)(2,1)S(1)}, bf16[128,2048]{1,0:T(8,128)(2,1)S(1)}, u32[]{:S(2)}, u32[]{:S(2)}) collective-permute-start(bf16[128,2048]{1,0:T(8,128)(2,1)S(1)} %get-tuple-element.12), channel_id=1, source_target_pairs={{16,0},{17,1},{18,2},{19,3},{20,4},{21,5},{22,6},{23,7},{24,8},{25... | collective-permute-start | bytes 1572872 | tf_op jit(solution)/shard_map/ppermute | solution.py:42
  142.1 17.8 %collective-permute-start.36 = (bf16[128,512]{0,1:T(8,128)(2,1)S(1)}, bf16[128,512]{0,1:T(8,128)(2,1)S(1)}, u32[]{:S(2)}, u32[]{:S(2)}) collective-permute-start(bf16[128,512]{0,1:T(8,128)(2,1)S(1)} %get-tuple-element.41), channel_id=1, source_target_pairs={{0,4},{1,5},{2,6},{3,7},{4,0},{5,1},{6,2},{7,3},{8,12},{9,13},{10,... | collective-permute-start | bytes 393224 | tf_op jit(solution)/shard_map/ppermute | solution.py:42
  143.8 16.1 %collective-permute-start.37 = (bf16[128,512]{0,1:T(8,128)(2,1)S(1)}, bf16[128,512]{0,1:T(8,128)(2,1)S(1)}, u32[]{:S(2)}, u32[]{:S(2)}) collective-permute-start(bf16[128,512]{0,1:T(8,128)(2,1)S(1)} %get-tuple-element.43), channel_id=1, source_target_pairs={{0,12},{1,13},{2,14},{3,15},{4,8},{5,9},{6,10},{7,11},{8,4},{9,5},... | collective-permute-start | bytes 393224 | tf_op jit(solution)/shard_map/ppermute | solution.py:42
  146.8 13.1 %collective-permute-start.38 = (bf16[128,512]{0,1:T(8,128)(2,1)S(1)}, bf16[128,512]{0,1:T(8,128)(2,1)S(1)}, u32[]{:S(2)}, u32[]{:S(2)}) collective-permute-start(bf16[128,512]{0,1:T(8,128)(2,1)S(1)} %get-tuple-element.42), channel_id=1, source_target_pairs={{0,8},{1,9},{2,10},{3,11},{4,12},{5,13},{6,14},{7,15},{8,0},{9,1},... | collective-permute-start | bytes 393224 | tf_op jit(solution)/shard_map/ppermute | solution.py:42
  164.7 20.5 %collective-permute-start.44 = (bf16[128,512]{1,0:T(8,128)(2,1)S(1)}, bf16[128,512]{1,0:T(8,128)(2,1)S(1)}, u32[]{:S(2)}, u32[]{:S(2)}) collective-permute-start(bf16[128,512]{1,0:T(8,128)(2,1)S(1)} %get-tuple-element.34), channel_id=1, source_target_pairs={{0,12},{1,13},{2,14},{3,15},{4,8},{5,9},{6,10},{7,11},{8,4},{9,5},... | collective-permute-start | bytes 393224 | tf_op jit(solution)/shard_map/ppermute | solution.py:42
  170.2 15.0 %collective-permute-start.45 = (bf16[128,512]{1,0:T(8,128)(2,1)S(1)}, bf16[128,512]{1,0:T(8,128)(2,1)S(1)}, u32[]{:S(2)}, u32[]{:S(2)}) collective-permute-start(bf16[128,512]{1,0:T(8,128)(2,1)S(1)} %get-tuple-element.33), channel_id=1, source_target_pairs={{0,8},{1,9},{2,10},{3,11},{4,12},{5,13},{6,14},{7,15},{8,0},{9,1},... | collective-permute-start | bytes 393224 | tf_op jit(solution)/shard_map/ppermute | solution.py:42
  170.5 12.3 %collective-permute-start.43 = (bf16[128,512]{1,0:T(8,128)(2,1)S(1)}, bf16[128,512]{1,0:T(8,128)(2,1)S(1)}, u32[]{:S(2)}, u32[]{:S(2)}) collective-permute-start(bf16[128,512]{1,0:T(8,128)(2,1)S(1)} %get-tuple-element.36), channel_id=1, source_target_pairs={{0,4},{1,5},{2,6},{3,7},{4,0},{5,1},{6,2},{7,3},{8,12},{9,13},{10,... | collective-permute-start | bytes 393224 | tf_op jit(solution)/shard_map/ppermute | solution.py:42
  176.6 26.3 %collective-permute-start.42 = (bf16[128,2048]{1,0:T(8,128)(2,1)S(1)}, bf16[128,2048]{1,0:T(8,128)(2,1)S(1)}, u32[]{:S(2)}, u32[]{:S(2)}) collective-permute-start(bf16[128,2048]{1,0:T(8,128)(2,1)S(1)} %get-tuple-element.16), channel_id=1, source_target_pairs={{16,0},{17,1},{18,2},{19,3},{20,4},{21,5},{22,6},{23,7},{24,8},{25... | collective-permute-start | bytes 1572872 | tf_op jit(solution)/shard_map/ppermute | solution.py:42
  178.0 24.9 %collective-permute-start.41 = (bf16[144,2048]{1,0:T(8,128)(2,1)S(1)}, bf16[144,2048]{1,0:T(8,128)(2,1)S(1)}, u32[]{:S(2)}, u32[]{:S(2)}) collective-permute-start(bf16[144,2048]{1,0:T(8,128)(2,1)S(1)} %pad_maximum_fusion.4), channel_id=1, source_target_pairs={{0,16},{1,17},{2,18},{3,19},{4,20},{5,21},{6,22},{7,23},{8,24},{9,... | collective-permute-start | bytes 1769480 | tf_op jit(solution)/shard_map/ppermute | solution.py:42
  185.2 10.8 %collective-permute-start.48 = (bf16[2,128,512]{2,1,0:T(8,128)(2,1)S(1)}, bf16[2,128,512]{2,1,0:T(8,128)(2,1)S(1)}, u32[]{:S(2)}, u32[]{:S(2)}) collective-permute-start(bf16[2,128,512]{2,1,0:T(8,128)(2,1)S(1)} %maximum_select_fusion.16), channel_id=1, source_target_pairs={{0,1},{1,0},{2,3},{3,2},{4,5},{5,4},{6,7},{7,6},{8,9},{9,8},{10,11... | collective-permute-start | bytes 786440 | tf_op jit(solution)/shard_map/ppermute | solution.py:42
  185.2 10.8 %collective-permute-start.47 = (bf16[2,128,512]{2,1,0:T(8,128)(2,1)S(1)}, bf16[2,128,512]{2,1,0:T(8,128)(2,1)S(1)}, u32[]{:S(2)}, u32[]{:S(2)}) collective-permute-start(bf16[2,128,512]{2,1,0:T(8,128)(2,1)S(1)} %maximum_select_fusion.17), channel_id=1, source_target_pairs={{0,2},{1,3},{2,0},{3,1},{4,6},{5,7},{6,4},{7,5},{8,10},{9,11},{10,... | collective-permute-start | bytes 786440 | tf_op jit(solution)/shard_map/ppermute | solution.py:42
  199.3 11.6 %collective-permute-start.52 = (bf16[128,512]{0,1:T(8,128)(2,1)S(1)}, bf16[128,512]{0,1:T(8,128)(2,1)S(1)}, u32[]{:S(2)}, u32[]{:S(2)}) collective-permute-start(bf16[128,512]{0,1:T(8,128)(2,1)S(1)} %get-tuple-element.28), channel_id=1, source_target_pairs={{0,4},{1,5},{2,6},{3,7},{4,0},{5,1},{6,2},{7,3},{8,12},{9,13},{10,... | collective-permute-start | bytes 393224 | tf_op jit(solution)/shard_map/ppermute | solution.py:42
  200.0 11.0 %collective-permute-start.53 = (bf16[128,512]{0,1:T(8,128)(2,1)S(1)}, bf16[128,512]{0,1:T(8,128)(2,1)S(1)}, u32[]{:S(2)}, u32[]{:S(2)}) collective-permute-start(bf16[128,512]{0,1:T(8,128)(2,1)S(1)} %get-tuple-element.30), channel_id=1, source_target_pairs={{0,12},{1,13},{2,14},{3,15},{4,8},{5,9},{6,10},{7,11},{8,4},{9,5},... | collective-permute-start | bytes 393224 | tf_op jit(solution)/shard_map/ppermute | solution.py:42
  202.6 12.1 %collective-permute-start.54 = (bf16[128,512]{0,1:T(8,128)(2,1)S(1)}, bf16[128,512]{0,1:T(8,128)(2,1)S(1)}, u32[]{:S(2)}, u32[]{:S(2)}) collective-permute-start(bf16[128,512]{0,1:T(8,128)(2,1)S(1)} %get-tuple-element.29), channel_id=1, source_target_pairs={{0,8},{1,9},{2,10},{3,11},{4,12},{5,13},{6,14},{7,15},{8,0},{9,1},... | collective-permute-start | bytes 393224 | tf_op jit(solution)/shard_map/ppermute | solution.py:42
  (32 other events, 244.4 us)

commit v2 on v1

--- a/solution.py
+++ b/solution.py
@@ -155,7 +155,7 @@
             pltpu.roll(above, 1, 0) + pltpu.roll(below, deep - 1, 0) + left + right - 4.0 * here
         )
 
-    together = max(n for n in (1, 2, 3) if blocks % n == 0)
+    together = max(n for n in (1, 2, 3, 6) if blocks % n == 0)
 
     def each_block(body):
         def several(trip, carry):
@@ -248,30 +248,24 @@
             name="begin",
         )(ends, incr, diffuse, before, after)
 
-    def update_body(
-        ends_ref, coef, past, arrived, pulled, mult, following, incr, forcing_ref,
-        past_new, incr_new, target, grad, one, two
-    ):
+    def update_body(ends_ref, coef, past, arrived, pulled, past_new, moved, one, two):
         clear_rims(one, two)
         past_new[...] = past[...] + step_weight * (
             arrived[...].astype(f32) - ends_ref[2] * pulled[...]
         )
         one[inside] = past_new[...]
-        slope = mult[...] - following[...].astype(f32)
-        grad[...] = slope
-        incr_new[...] = incr[...] + step_weight * slope
-        target[...] = forcing_ref[...] - incr_new[...] + propagate(ends_ref, coef, one, two)
-
-    def update(past, arrived, pulled, mult, following, incr):
+        moved[...] = propagate(ends_ref, coef, one, two)
+
+    def update(past, arrived, pulled):
         return pl.pallas_call(
             update_body,
-            out_shape=[wide_f32, field_f32, field_f32, field_f32],
-            in_specs=[scalars] + [whole] * 8,
-            out_specs=[whole] * 4,
+            out_shape=[wide_f32, field_f32],
+            in_specs=[scalars] + [whole] * 4,
+            out_specs=[whole] * 2,
             scratch_shapes=[padded, padded],
             compiler_params=limits,
             name="update",
-        )(ends, diffuse_wide, past, arrived, pulled, mult, following, incr, forcing)
+        )(ends, diffuse_wide, past, arrived, pulled)
 
     short = jnp.concatenate(
         [diffuse.astype(jnp.bfloat16), incr_start[0].astype(jnp.bfloat16)], axis=0
@@ -301,9 +295,10 @@
         following = to_sub(middle, -1)
         arrived = to_sub(jnp.concatenate([above, low, below], axis=0), 1)
         tile = product(spread(pieces))
-        past_wide, incr, target, grad = update(
-            past_wide, arrived, pulled, multiplier, following, incr
-        )
+        past_wide, moved = update(past_wide, arrived, pulled)
+        grad = multiplier - following.astype(f32)
+        incr = incr + step_weight * grad
+        target = forcing - incr + moved
         return target, multiplier, incr, past_wide, tile, grad
 
     multiplier = mult_start[0]
@@ -314,6 +309,7 @@
         target, multiplier, incr, past_wide, tile, grad = advance(
             target, multiplier, incr, past_wide, tile
         )
+    target, grad = lax.optimization_barrier((target, grad))
     mult_resid = target - finish(tile)
     return (mult_resid[None], grad[None])
 

time: 218 us -> 214 us (0.982)
  starting transfers between devices: 75.4 us -> 82.6 us
  waiting for transfers between devices: 84 us -> 77.1 us
  Pallas kernels: 32.6 us -> 25.8 us
  other arithmetic: 6.78 us -> 9.4 us
    ppermute x55, starting transfers between devices: 75.4 us -> 82.6 us  [send(): return lax.ppermute(value, BOTH, pairs)]
    ppermute x55, waiting for transfers between devices: 84 us -> 77.1 us  [send(): return lax.ppermute(value, BOTH, pairs)]
    pallas_call x2, Pallas kernels: 15.4 us -> 11.1 us  [update(): pl.pallas_call(update_body, out_shape=[wide_f32, field_f32], in_specs=[sc...]
  transfers between devices with their start and end apart: 55 -> 55, of which waited for: 21 -> 19; matrix products, arithmetic and copies ran while one was open for 8% -> 10% of each run, Pallas kernels for 15% -> 12%
where the time goes in v2:
time: 214 us
  starting transfers between devices  82.6 us (39%)
  waiting for transfers between devices  77.1 us (36%)
  Pallas kernels  25.8 us (12%)
  other arithmetic  9.4 us (4%)
  local copies, waits for them, and re-layouts  9.03 us (4%)
  matrix products  8.22 us (4%)
    ppermute x55, starting transfers between devices, send(): return lax.ppermute(value, BOTH, pairs)  82.6 us
    ppermute x55, waiting for transfers between devices, send(): return lax.ppermute(value, BOTH, pairs)  77.1 us
    pallas_call x2, Pallas kernels, update(): pl.pallas_call(update_body, out_shape=[wide_f32, field_f32], in_specs=[sc...  11.1 us
    pallas_call x2, Pallas kernels, adjoint(): pl.pallas_call(adjoint_body, out_shape=[wide_f32, field_bf16], in_specs=[...  9.85 us
    pallas_call x1, Pallas kernels, begin(): pl.pallas_call(begin_body, out_shape=field_bf16, in_specs=[scalars] + [wh...  4.82 us
    dot_general x3, matrix products, finish(): return jnp.dot(line, east_corr, preferred_element_type=jnp.float32)  4.35 us
  transfers between devices with their start and end apart: 55, of which 19 were waited for; matrix products, arithmetic and copies ran while one was open for 10% of the time, Pallas kernels for 12%

profile of v2, /device:TPU:0, one launch (start us, length us, event | category | flops | bytes accessed | tf_op | source)
XLA Modules:
  0.0 213.9 jit_solution(15022187015428831080)
XLA Ops:
  2.5 3.1 %collective-permute-start.3 = (bf16[64,2048]{1,0:T(8,128)(2,1)}, bf16[64,2048]{1,0:T(8,128)(2,1)}, u32[]{:S(2)}, u32[]{:S(2)}) collective-permute-start(bf16[64,2048]{1,0:T(8,128)(2,1)} %constant_dynamic-slice_fusion.9), channel_id=1, source_target_pairs={{0,4},{1,5},{2,6},{3,7},{4,0},{5,1},{6,2},{7,3},{8,12},{9,13},{10,... | collective-permute-start | bytes 786440 | tf_op jit(solution)/shard_map/ppermute | solution.py:42
  5.5 2.6 %collective-permute-start.5 = (bf16[64,2048]{1,0:T(8,128)(2,1)}, bf16[64,2048]{1,0:T(8,128)(2,1)}, u32[]{:S(2)}, u32[]{:S(2)}) collective-permute-start(bf16[64,2048]{1,0:T(8,128)(2,1)} %constant_dynamic-slice_fusion.9), channel_id=1, source_target_pairs={{0,8},{1,9},{2,10},{3,11},{4,12},{5,13},{6,14},{7,15},{8,0},{9,1},... | collective-permute-start | bytes 786440 | tf_op jit(solution)/shard_map/ppermute | solution.py:42
  14.5 4.3 %collective-permute-start.9 = (bf16[128,512]{1,0:T(8,128)(2,1)}, bf16[128,512]{1,0:T(8,128)(2,1)S(1)}, u32[]{:S(2)}, u32[]{:S(2)}) collective-permute-start(bf16[128,512]{1,0:T(8,128)(2,1)} %get-tuple-element.64), channel_id=1, source_target_pairs={{0,4},{1,5},{2,6},{3,7},{4,0},{5,1},{6,2},{7,3},{8,12},{9,13},{10,... | collective-permute-start | bytes 393224 | tf_op jit(solution)/shard_map/ppermute | solution.py:42
  18.8 2.4 %pad_maximum_fusion.2 = bf16[256,2048]{1,0:T(8,128)(2,1)} fusion(bf16[128,2048]{1,0:T(8,128)(2,1)} %copy-done.5, bf16[128,2048]{1,0:T(8,128)(2,1)} %copy-done.4), kind=kLoop, calls=%fused_computation.5 | loop fusion | flops 2097152 | bytes 2097152 | tf_op jit(solution)/shard_map/concatenate | solution.py:270
  21.2 2.6 %dynamic_update_slice.93 = bf16[512,2048]{1,0:T(8,128)(2,1)} pad(bf16[128,2048]{1,0:T(8,128)(2,1)} %param.10, bf16[]{:T(256)} %constant.206.clone.1), padding=0_384x0_0 | pad | bytes 2621442 | tf_op jit(solution)/shard_map/dynamic_update_slice | solution.py:80
  26.2 4.8 %begin.1 = bf16[128,2048]{1,0:T(8,128)(2,1)S(1)} custom-call(f32[3]{0:T(128)S(1)} %add_convert_fusion.ends_ref, f32[128,2048]{1,0:T(8,128)S(1)} %bitcast.184, f32[128,2048]{1,0:T(8,128)S(1)} %bitcast.185, bf16[16,2048]{1,0:T(8,128)(2,1)S(1)} %collective-permute-done.before, bf16[16,2048]{1,0:T(8,128)(2,1)S(1)} %collective-permute-done.1.after), custom_call_target="tpu_custom_call" | custom-call | tf_op jit(solution)/shard_map/begin/pallas_call | solution.py:241
  31.1 3.5 %collective-permute-start.24 = (bf16[256,2048]{1,0:T(8,128)(2,1)S(1)}, bf16[256,2048]{1,0:T(8,128)(2,1)S(1)}, u32[]{:S(2)}, u32[]{:S(2)}) collective-permute-start(bf16[256,2048]{1,0:T(8,128)(2,1)S(1)} %copy-done.7), channel_id=1, source_target_pairs={{0,16},{1,17},{2,18},{3,19},{4,20},{5,21},{6,22},{7,23},{8,24},{9,... | collective-permute-start | bytes 3145736 | tf_op jit(solution)/shard_map/ppermute | solution.py:42
  35.8 3.4 %collective-permute-start.2 = (bf16[128,2048]{1,0:T(8,128)(2,1)S(1)}, bf16[128,2048]{1,0:T(8,128)(2,1)S(1)}, u32[]{:S(2)}, u32[]{:S(2)}) collective-permute-start(bf16[128,2048]{1,0:T(8,128)(2,1)S(1)} %begin.1), channel_id=1, source_target_pairs={{0,16},{1,17},{2,18},{3,19},{4,20},{5,21},{6,22},{7,23},{8,24},{9,... | collective-permute-start | bytes 1572872 | tf_op jit(solution)/shard_map/ppermute | solution.py:42
  42.7 5.2 %collective-permute-done.12 = bf16[2,128,512]{2,1,0:T(8,128)(2,1)S(1)} collective-permute-done((bf16[2,128,512]{2,1,0:T(8,128)(2,1)S(1)}, bf16[2,128,512]{2,1,0:T(8,128)(2,1)S(1)}, u32[]{:S(2)}, u32[]{:S(2)}) %collective-permute-start.12) | collective-permute-done | bytes 262176 | tf_op jit(solution)/shard_map/ppermute | solution.py:42
  48.0 2.8 %collective-permute-done.13 = bf16[2,128,512]{2,1,0:T(8,128)(2,1)S(1)} collective-permute-done((bf16[2,128,512]{2,1,0:T(8,128)(2,1)S(1)}, bf16[2,128,512]{2,1,0:T(8,128)(2,1)S(1)}, u32[]{:S(2)}, u32[]{:S(2)}) %collective-permute-start.13) | collective-permute-done | bytes 262176 | tf_op jit(solution)/shard_map/ppermute | solution.py:42
  50.9 3.9 %collective-permute-start.23 = (bf16[32,2048]{1,0:T(8,128)(2,1)S(1)}, bf16[32,2048]{1,0:T(8,128)(2,1)S(1)}, u32[]{:S(2)}, u32[]{:S(2)}) collective-permute-start(bf16[32,2048]{1,0:T(8,128)(2,1)S(1)} %pad_maximum_fusion.5), channel_id=1, source_target_pairs={{0,16},{1,17},{2,18},{3,19},{4,20},{5,21},{6,22},{7,23},{8,24},{9,... | collective-permute-start | bytes 393224 | tf_op jit(solution)/shard_map/ppermute | solution.py:42
  55.0 20.0 %collective-permute-done.4 = bf16[64,2048]{1,0:T(8,128)(2,1)S(1)} collective-permute-done((bf16[64,2048]{1,0:T(8,128)(2,1)}, bf16[64,2048]{1,0:T(8,128)(2,1)S(1)}, u32[]{:S(2)}, u32[]{:S(2)}) %collective-permute-start.4) | collective-permute-done | bytes 262176 | tf_op jit(solution)/shard_map/ppermute | solution.py:42
  77.1 5.1 %collective-permute-done.6 = bf16[64,2048]{1,0:T(8,128)(2,1)S(1)} collective-permute-done((bf16[64,2048]{1,0:T(8,128)(2,1)}, bf16[64,2048]{1,0:T(8,128)(2,1)S(1)}, u32[]{:S(2)}, u32[]{:S(2)}) %collective-permute-start.6) | collective-permute-done | bytes 262176 | tf_op jit(solution)/shard_map/ppermute | solution.py:42
  83.7 2.4 %collective-permute-start.8 = (bf16[64,2048]{1,0:T(8,128)(2,1)S(1)}, bf16[64,2048]{1,0:T(8,128)(2,1)S(1)}, u32[]{:S(2)}, u32[]{:S(2)}) collective-permute-start(bf16[64,2048]{1,0:T(8,128)(2,1)S(1)} %collective-permute-done.7), channel_id=1, source_target_pairs={{0,16},{1,17},{2,18},{3,19},{4,20},{5,21},{6,22},{7,23},{8,24},{9,... | collective-permute-start | bytes 786440 | tf_op jit(solution)/shard_map/ppermute | solution.py:42
  86.2 6.5 %collective-permute-done.8 = bf16[64,2048]{1,0:T(8,128)(2,1)S(1)} collective-permute-done((bf16[64,2048]{1,0:T(8,128)(2,1)S(1)}, bf16[64,2048]{1,0:T(8,128)(2,1)S(1)}, u32[]{:S(2)}, u32[]{:S(2)}) %collective-permute-start.8) | collective-permute-done | bytes 262176 | tf_op jit(solution)/shard_map/ppermute | solution.py:42
  97.7 7.1 %collective-permute-done.20 = bf16[128,512]{0,1:T(8,128)(2,1)S(1)} collective-permute-done((bf16[128,512]{0,1:T(8,128)(2,1)S(1)}, bf16[128,512]{0,1:T(8,128)(2,1)S(1)}, u32[]{:S(2)}, u32[]{:S(2)}) %collective-permute-start.20) | collective-permute-done | bytes 131104 | tf_op jit(solution)/shard_map/ppermute | solution.py:42
  109.3 3.0 %collective-permute-start.21 = (bf16[8,2048]{1,0:T(8,128)(2,1)S(1)}, bf16[8,2048]{1,0:T(8,128)(2,1)S(1)}, u32[]{:S(2)}, u32[]{:S(2)}) collective-permute-start(bf16[8,2048]{1,0:T(8,128)(2,1)S(1)} %get-tuple-element.52), channel_id=1, source_target_pairs={{0,1},{1,2},{2,3},{3,4},{4,5},{5,6},{6,7},{7,8},{8,9},{9,10},{10,1... | collective-permute-start | bytes 98312 | tf_op jit(solution)/shard_map/ppermute | solution.py:42
  117.3 3.4 %collective-permute-start.26 = (bf16[144,2048]{1,0:T(8,128)(2,1)S(1)}, bf16[144,2048]{1,0:T(8,128)(2,1)S(1)}, u32[]{:S(2)}, u32[]{:S(2)}) collective-permute-start(bf16[144,2048]{1,0:T(8,128)(2,1)S(1)} %pad_maximum_fusion.3), channel_id=1, source_target_pairs={{0,16},{1,17},{2,18},{3,19},{4,20},{5,21},{6,22},{7,23},{8,24},{9,... | collective-permute-start | bytes 1769480 | tf_op jit(solution)/shard_map/ppermute | solution.py:42
  121.8 5.4 %collective-permute-done.29 = bf16[128,512]{1,0:T(8,128)(2,1)S(1)} collective-permute-done((bf16[128,512]{1,0:T(8,128)(2,1)S(1)}, bf16[128,512]{1,0:T(8,128)(2,1)S(1)}, u32[]{:S(2)}, u32[]{:S(2)}) %collective-permute-start.29) | collective-permute-done | bytes 131104 | tf_op jit(solution)/shard_map/ppermute | solution.py:42
  129.4 4.9 %adjoint.2 = (f32[144,2048]{1,0:T(8,128)S(1)}, bf16[128,2048]{1,0:T(8,128)(2,1)S(1)}) custom-call(f32[3]{0:T(128)S(1)} %add_convert_fusion.ends_ref, f32[128,2048]{1,0:T(8,128)S(1)} %get-tuple-element.23.mult, bf16[8,2048]{1,0:T(8,128)(2,1)S(1)} %collective-permute-done.21.above, bf16[8,2048]{1,0:T(8,128)(2,1)S(1)} %collective-permute-done.22.below, ...), custom_call_target="tpu_custom_call" | custom-call | tf_op jit(solution)/shard_map/adjoint/pallas_call | solution.py:205
  139.5 2.4 %collective-permute-start.38 = (bf16[128,512]{0,1:T(8,128)(2,1)S(1)}, bf16[128,512]{0,1:T(8,128)(2,1)S(1)}, u32[]{:S(2)}, u32[]{:S(2)}) collective-permute-start(bf16[128,512]{0,1:T(8,128)(2,1)S(1)} %get-tuple-element.44), channel_id=1, source_target_pairs={{0,8},{1,9},{2,10},{3,11},{4,12},{5,13},{6,14},{7,15},{8,0},{9,1},... | collective-permute-start | bytes 393224 | tf_op jit(solution)/shard_map/ppermute | solution.py:42
  141.9 2.8 %collective-permute-start.37 = (bf16[128,512]{0,1:T(8,128)(2,1)S(1)}, bf16[128,512]{0,1:T(8,128)(2,1)S(1)}, u32[]{:S(2)}, u32[]{:S(2)}) collective-permute-start(bf16[128,512]{0,1:T(8,128)(2,1)S(1)} %get-tuple-element.45), channel_id=1, source_target_pairs={{0,12},{1,13},{2,14},{3,15},{4,8},{5,9},{6,10},{7,11},{8,4},{9,5},... | collective-permute-start | bytes 393224 | tf_op jit(solution)/shard_map/ppermute | solution.py:42
  144.8 5.1 %update.2 = (f32[144,2048]{1,0:T(8,128)S(1)}, f32[128,2048]{1,0:T(8,128)S(1)}) custom-call(f32[3]{0:T(128)S(1)} %add_convert_fusion.ends_ref, f32[144,2048]{1,0:T(8,128)S(1)} %pad_maximum_fusion.coef, f32[144,2048]{1,0:T(8,128)S(1)} %pad_maximum_fusion.1.past, bf16[144,2048]{1,0:T(8,128)(2,1)S(1)} %collective-permute-done.26.arrived, ...), custom_call_target="tpu_custom_call" | custom-call | tf_op jit(solution)/shard_map/update/pallas_call | solution.py:260
  149.9 2.6 %collective-permute-done.38 = bf16[128,512]{0,1:T(8,128)(2,1)S(1)} collective-permute-done((bf16[128,512]{0,1:T(8,128)(2,1)S(1)}, bf16[128,512]{0,1:T(8,128)(2,1)S(1)}, u32[]{:S(2)}, u32[]{:S(2)}) %collective-permute-start.38) | collective-permute-done | bytes 131104 | tf_op jit(solution)/shard_map/ppermute | solution.py:42
  157.8 5.9 %collective-permute-start.43 = (bf16[128,512]{1,0:T(8,128)(2,1)S(1)}, bf16[128,512]{1,0:T(8,128)(2,1)S(1)}, u32[]{:S(2)}, u32[]{:S(2)}) collective-permute-start(bf16[128,512]{1,0:T(8,128)(2,1)S(1)} %get-tuple-element.38), channel_id=1, source_target_pairs={{0,4},{1,5},{2,6},{3,7},{4,0},{5,1},{6,2},{7,3},{8,12},{9,13},{10,... | collective-permute-start | bytes 393224 | tf_op jit(solution)/shard_map/ppermute | solution.py:42
  166.3 4.9 %adjoint.3 = (f32[144,2048]{1,0:T(8,128)S(1)}, bf16[128,2048]{1,0:T(8,128)(2,1)S(1)}) custom-call(f32[3]{0:T(128)S(1)} %add_convert_fusion.ends_ref, f32[128,2048]{1,0:T(8,128)S(1)} %get-tuple-element.21.mult, bf16[8,2048]{1,0:T(8,128)(2,1)S(1)} %collective-permute-done.39.above, bf16[8,2048]{1,0:T(8,128)(2,1)S(1)} %collective-permute-done.40.below, ...), custom_call_target="tpu_custom_call" | custom-call | tf_op jit(solution)/shard_map/adjoint/pallas_call | solution.py:205
  172.6 4.8 %collective-permute-start.42 = (bf16[144,2048]{1,0:T(8,128)(2,1)S(1)}, bf16[144,2048]{1,0:T(8,128)(2,1)S(1)}, u32[]{:S(2)}, u32[]{:S(2)}) collective-permute-start(bf16[144,2048]{1,0:T(8,128)(2,1)S(1)} %pad_maximum_fusion.4), channel_id=1, source_target_pairs={{0,16},{1,17},{2,18},{3,19},{4,20},{5,21},{6,22},{7,23},{8,24},{9,... | collective-permute-start | bytes 1769480 | tf_op jit(solution)/shard_map/ppermute | solution.py:42
  180.0 6.7 %collective-permute-done.46 = bf16[2,128,512]{2,1,0:T(8,128)(2,1)S(1)} collective-permute-done((bf16[2,128,512]{2,1,0:T(8,128)(2,1)S(1)}, bf16[2,128,512]{2,1,0:T(8,128)(2,1)S(1)}, u32[]{:S(2)}, u32[]{:S(2)}) %collective-permute-start.46) | collective-permute-done | bytes 262176 | tf_op jit(solution)/shard_map/ppermute | solution.py:42
  186.8 2.8 %collective-permute-done.47 = bf16[2,128,512]{2,1,0:T(8,128)(2,1)S(1)} collective-permute-done((bf16[2,128,512]{2,1,0:T(8,128)(2,1)S(1)}, bf16[2,128,512]{2,1,0:T(8,128)(2,1)S(1)}, u32[]{:S(2)}, u32[]{:S(2)}) %collective-permute-start.47) | collective-permute-done | bytes 262176 | tf_op jit(solution)/shard_map/ppermute | solution.py:42
  190.3 6.0 %update.3 = (f32[144,2048]{1,0:T(8,128)}, f32[128,2048]{1,0:T(8,128)S(1)}) custom-call(f32[3]{0:T(128)S(1)} %add_convert_fusion.ends_ref, f32[144,2048]{1,0:T(8,128)S(1)} %pad_maximum_fusion.coef, f32[144,2048]{1,0:T(8,128)S(1)} %get-tuple-element.15.past, bf16[144,2048]{1,0:T(8,128)(2,1)S(1)} %collective-permute-done.42.arrived, ...), custom_call_target="tpu_custom_call" | custom-call | tf_op jit(solution)/shard_map/update/pallas_call | solution.py:260
  199.8 2.6 %collective-permute-start.53 = (bf16[128,512]{0,1:T(8,128)(2,1)S(1)}, bf16[128,512]{0,1:T(8,128)(2,1)S(1)}, u32[]{:S(2)}, u32[]{:S(2)}) collective-permute-start(bf16[128,512]{0,1:T(8,128)(2,1)S(1)} %get-tuple-element.32), channel_id=1, source_target_pairs={{0,12},{1,13},{2,14},{3,15},{4,8},{5,9},{6,10},{7,11},{8,4},{9,5},... | collective-permute-start | bytes 393224 | tf_op jit(solution)/shard_map/ppermute | solution.py:42
  203.9 6.9 %collective-permute-done.54 = bf16[128,512]{0,1:T(8,128)(2,1)S(1)} collective-permute-done((bf16[128,512]{0,1:T(8,128)(2,1)S(1)}, bf16[128,512]{0,1:T(8,128)(2,1)S(1)}, u32[]{:S(2)}, u32[]{:S(2)}) %collective-permute-start.54) | collective-permute-done | bytes 131104 | tf_op jit(solution)/shard_map/ppermute | solution.py:42
  (187 shorter events, 62.3 us)
Async XLA Ops:
  2.5 37.6 %collective-permute-start.3 = (bf16[64,2048]{1,0:T(8,128)(2,1)}, bf16[64,2048]{1,0:T(8,128)(2,1)}, u32[]{:S(2)}, u32[]{:S(2)}) collective-permute-start(bf16[64,2048]{1,0:T(8,128)(2,1)} %constant_dynamic-slice_fusion.9), channel_id=1, source_target_pairs={{0,4},{1,5},{2,6},{3,7},{4,0},{5,1},{6,2},{7,3},{8,12},{9,13},{10,... | collective-permute-start | bytes 786440 | tf_op jit(solution)/shard_map/ppermute | solution.py:42
  5.5 45.4 %collective-permute-start.5 = (bf16[64,2048]{1,0:T(8,128)(2,1)}, bf16[64,2048]{1,0:T(8,128)(2,1)}, u32[]{:S(2)}, u32[]{:S(2)}) collective-permute-start(bf16[64,2048]{1,0:T(8,128)(2,1)} %constant_dynamic-slice_fusion.9), channel_id=1, source_target_pairs={{0,8},{1,9},{2,10},{3,11},{4,12},{5,13},{6,14},{7,15},{8,0},{9,1},... | collective-permute-start | bytes 786440 | tf_op jit(solution)/shard_map/ppermute | solution.py:42
  10.3 13.6 %collective-permute-start = (bf16[16,2048]{1,0:T(8,128)(2,1)}, bf16[16,2048]{1,0:T(8,128)(2,1)S(1)}, u32[]{:S(2)}, u32[]{:S(2)}) collective-permute-start(bf16[16,2048]{1,0:T(8,128)(2,1)} %pad_maximum_fusion.6), channel_id=1, source_target_pairs={{0,1},{1,2},{2,3},{3,4},{4,5},{5,6},{6,7},{7,8},{8,9},{9,10},{10,1... | collective-permute-start | bytes 196616 | tf_op jit(solution)/shard_map/ppermute | solution.py:42
  12.2 11.6 %collective-permute-start.1 = (bf16[16,2048]{1,0:T(8,128)(2,1)}, bf16[16,2048]{1,0:T(8,128)(2,1)S(1)}, u32[]{:S(2)}, u32[]{:S(2)}) collective-permute-start(bf16[16,2048]{1,0:T(8,128)(2,1)} %pad_maximum_fusion.7), channel_id=1, source_target_pairs={{1,0},{2,1},{3,2},{4,3},{5,4},{6,5},{7,6},{8,7},{9,8},{10,9},{11,1... | collective-permute-start | bytes 196616 | tf_op jit(solution)/shard_map/ppermute | solution.py:42
  14.5 16.6 %collective-permute-start.9 = (bf16[128,512]{1,0:T(8,128)(2,1)}, bf16[128,512]{1,0:T(8,128)(2,1)S(1)}, u32[]{:S(2)}, u32[]{:S(2)}) collective-permute-start(bf16[128,512]{1,0:T(8,128)(2,1)} %get-tuple-element.64), channel_id=1, source_target_pairs={{0,4},{1,5},{2,6},{3,7},{4,0},{5,1},{6,2},{7,3},{8,12},{9,13},{10,... | collective-permute-start | bytes 393224 | tf_op jit(solution)/shard_map/ppermute | solution.py:42
  23.8 12.0 %collective-permute-start.11 = (bf16[128,512]{1,0:T(8,128)(2,1)}, bf16[128,512]{1,0:T(8,128)(2,1)S(1)}, u32[]{:S(2)}, u32[]{:S(2)}) collective-permute-start(bf16[128,512]{1,0:T(8,128)(2,1)} %get-tuple-element.61), channel_id=1, source_target_pairs={{0,8},{1,9},{2,10},{3,11},{4,12},{5,13},{6,14},{7,15},{8,0},{9,1},... | collective-permute-start | bytes 393224 | tf_op jit(solution)/shard_map/ppermute | solution.py:42
  23.9 15.4 %collective-permute-start.10 = (bf16[128,512]{1,0:T(8,128)(2,1)}, bf16[128,512]{1,0:T(8,128)(2,1)S(1)}, u32[]{:S(2)}, u32[]{:S(2)}) collective-permute-start(bf16[128,512]{1,0:T(8,128)(2,1)} %get-tuple-element.62), channel_id=1, source_target_pairs={{0,12},{1,13},{2,14},{3,15},{4,8},{5,9},{6,10},{7,11},{8,4},{9,5},... | collective-permute-start | bytes 393224 | tf_op jit(solution)/shard_map/ppermute | solution.py:42
  31.1 98.0 %collective-permute-start.24 = (bf16[256,2048]{1,0:T(8,128)(2,1)S(1)}, bf16[256,2048]{1,0:T(8,128)(2,1)S(1)}, u32[]{:S(2)}, u32[]{:S(2)}) collective-permute-start(bf16[256,2048]{1,0:T(8,128)(2,1)S(1)} %copy-done.7), channel_id=1, source_target_pairs={{0,16},{1,17},{2,18},{3,19},{4,20},{5,21},{6,22},{7,23},{8,24},{9,... | collective-permute-start | bytes 3145736 | tf_op jit(solution)/shard_map/ppermute | solution.py:42
  35.8 70.6 %collective-permute-start.2 = (bf16[128,2048]{1,0:T(8,128)(2,1)S(1)}, bf16[128,2048]{1,0:T(8,128)(2,1)S(1)}, u32[]{:S(2)}, u32[]{:S(2)}) collective-permute-start(bf16[128,2048]{1,0:T(8,128)(2,1)S(1)} %begin.1), channel_id=1, source_target_pairs={{0,16},{1,17},{2,18},{3,19},{4,20},{5,21},{6,22},{7,23},{8,24},{9,... | collective-permute-start | bytes 1572872 | tf_op jit(solution)/shard_map/ppermute | solution.py:42
  40.1 10.7 %collective-permute-start.13 = (bf16[2,128,512]{2,1,0:T(8,128)(2,1)S(1)}, bf16[2,128,512]{2,1,0:T(8,128)(2,1)S(1)}, u32[]{:S(2)}, u32[]{:S(2)}) collective-permute-start(bf16[2,128,512]{2,1,0:T(8,128)(2,1)S(1)} %maximum_select_fusion.9), channel_id=1, source_target_pairs={{0,2},{1,3},{2,0},{3,1},{4,6},{5,7},{6,4},{7,5},{8,10},{9,11},{10,... | collective-permute-start | bytes 786440 | tf_op jit(solution)/shard_map/ppermute | solution.py:42
  50.8 24.2 %collective-permute-start.4 = (bf16[64,2048]{1,0:T(8,128)(2,1)}, bf16[64,2048]{1,0:T(8,128)(2,1)S(1)}, u32[]{:S(2)}, u32[]{:S(2)}) collective-permute-start(bf16[64,2048]{1,0:T(8,128)(2,1)} %collective-permute-done.3), channel_id=1, source_target_pairs={{0,16},{1,17},{2,18},{3,19},{4,20},{5,21},{6,22},{7,23},{8,24},{9,... | collective-permute-start | bytes 786440 | tf_op jit(solution)/shard_map/ppermute | solution.py:42
  50.9 45.2 %collective-permute-start.23 = (bf16[32,2048]{1,0:T(8,128)(2,1)S(1)}, bf16[32,2048]{1,0:T(8,128)(2,1)S(1)}, u32[]{:S(2)}, u32[]{:S(2)}) collective-permute-start(bf16[32,2048]{1,0:T(8,128)(2,1)S(1)} %pad_maximum_fusion.5), channel_id=1, source_target_pairs={{0,16},{1,17},{2,18},{3,19},{4,20},{5,21},{6,22},{7,23},{8,24},{9,... | collective-permute-start | bytes 393224 | tf_op jit(solution)/shard_map/ppermute | solution.py:42
  54.9 27.3 %collective-permute-start.6 = (bf16[64,2048]{1,0:T(8,128)(2,1)}, bf16[64,2048]{1,0:T(8,128)(2,1)S(1)}, u32[]{:S(2)}, u32[]{:S(2)}) collective-permute-start(bf16[64,2048]{1,0:T(8,128)(2,1)} %collective-permute-done.5), channel_id=1, source_target_pairs={{0,16},{1,17},{2,18},{3,19},{4,20},{5,21},{6,22},{7,23},{8,24},{9,... | collective-permute-start | bytes 786440 | tf_op jit(solution)/shard_map/ppermute | solution.py:42
  94.1 10.7 %collective-permute-start.20 = (bf16[128,512]{0,1:T(8,128)(2,1)S(1)}, bf16[128,512]{0,1:T(8,128)(2,1)S(1)}, u32[]{:S(2)}, u32[]{:S(2)}) collective-permute-start(bf16[128,512]{0,1:T(8,128)(2,1)S(1)} %get-tuple-element.57), channel_id=1, source_target_pairs={{0,8},{1,9},{2,10},{3,11},{4,12},{5,13},{6,14},{7,15},{8,0},{9,1},... | collective-permute-start | bytes 393224 | tf_op jit(solution)/shard_map/ppermute | solution.py:42
  94.2 10.6 %collective-permute-start.19 = (bf16[128,512]{0,1:T(8,128)(2,1)S(1)}, bf16[128,512]{0,1:T(8,128)(2,1)S(1)}, u32[]{:S(2)}, u32[]{:S(2)}) collective-permute-start(bf16[128,512]{0,1:T(8,128)(2,1)S(1)} %get-tuple-element.58), channel_id=1, source_target_pairs={{0,12},{1,13},{2,14},{3,15},{4,8},{5,9},{6,10},{7,11},{8,4},{9,5},... | collective-permute-start | bytes 393224 | tf_op jit(solution)/shard_map/ppermute | solution.py:42
  114.4 12.7 %collective-permute-start.29 = (bf16[128,512]{1,0:T(8,128)(2,1)S(1)}, bf16[128,512]{1,0:T(8,128)(2,1)S(1)}, u32[]{:S(2)}, u32[]{:S(2)}) collective-permute-start(bf16[128,512]{1,0:T(8,128)(2,1)S(1)} %get-tuple-element.48), channel_id=1, source_target_pairs={{0,8},{1,9},{2,10},{3,11},{4,12},{5,13},{6,14},{7,15},{8,0},{9,1},... | collective-permute-start | bytes 393224 | tf_op jit(solution)/shard_map/ppermute | solution.py:42
  115.9 11.4 %collective-permute-start.28 = (bf16[128,512]{1,0:T(8,128)(2,1)S(1)}, bf16[128,512]{1,0:T(8,128)(2,1)S(1)}, u32[]{:S(2)}, u32[]{:S(2)}) collective-permute-start(bf16[128,512]{1,0:T(8,128)(2,1)S(1)} %get-tuple-element.49), channel_id=1, source_target_pairs={{0,12},{1,13},{2,14},{3,15},{4,8},{5,9},{6,10},{7,11},{8,4},{9,5},... | collective-permute-start | bytes 393224 | tf_op jit(solution)/shard_map/ppermute | solution.py:42
  117.3 27.5 %collective-permute-start.26 = (bf16[144,2048]{1,0:T(8,128)(2,1)S(1)}, bf16[144,2048]{1,0:T(8,128)(2,1)S(1)}, u32[]{:S(2)}, u32[]{:S(2)}) collective-permute-start(bf16[144,2048]{1,0:T(8,128)(2,1)S(1)} %pad_maximum_fusion.3), channel_id=1, source_target_pairs={{0,16},{1,17},{2,18},{3,19},{4,20},{5,21},{6,22},{7,23},{8,24},{9,... | collective-permute-start | bytes 1769480 | tf_op jit(solution)/shard_map/ppermute | solution.py:42
  120.8 13.6 %collective-permute-start.30 = (bf16[2,128,512]{2,1,0:T(8,128)(2,1)S(1)}, bf16[2,128,512]{2,1,0:T(8,128)(2,1)S(1)}, u32[]{:S(2)}, u32[]{:S(2)}) collective-permute-start(bf16[2,128,512]{2,1,0:T(8,128)(2,1)S(1)} %maximum_select_fusion.12), channel_id=1, source_target_pairs={{0,2},{1,3},{2,0},{3,1},{4,6},{5,7},{6,4},{7,5},{8,10},{9,11},{10,... | collective-permute-start | bytes 786440 | tf_op jit(solution)/shard_map/ppermute | solution.py:42
  134.4 19.2 %collective-permute-start.25 = (bf16[128,2048]{1,0:T(8,128)(2,1)S(1)}, bf16[128,2048]{1,0:T(8,128)(2,1)S(1)}, u32[]{:S(2)}, u32[]{:S(2)}) collective-permute-start(bf16[128,2048]{1,0:T(8,128)(2,1)S(1)} %get-tuple-element.11), channel_id=1, source_target_pairs={{16,0},{17,1},{18,2},{19,3},{20,4},{21,5},{22,6},{23,7},{24,8},{25... | collective-permute-start | bytes 1572872 | tf_op jit(solution)/shard_map/ppermute | solution.py:42
  139.5 13.0 %collective-permute-start.38 = (bf16[128,512]{0,1:T(8,128)(2,1)S(1)}, bf16[128,512]{0,1:T(8,128)(2,1)S(1)}, u32[]{:S(2)}, u32[]{:S(2)}) collective-permute-start(bf16[128,512]{0,1:T(8,128)(2,1)S(1)} %get-tuple-element.44), channel_id=1, source_target_pairs={{0,8},{1,9},{2,10},{3,11},{4,12},{5,13},{6,14},{7,15},{8,0},{9,1},... | collective-permute-start | bytes 393224 | tf_op jit(solution)/shard_map/ppermute | solution.py:42
  141.9 10.6 %collective-permute-start.37 = (bf16[128,512]{0,1:T(8,128)(2,1)S(1)}, bf16[128,512]{0,1:T(8,128)(2,1)S(1)}, u32[]{:S(2)}, u32[]{:S(2)}) collective-permute-start(bf16[128,512]{0,1:T(8,128)(2,1)S(1)} %get-tuple-element.45), channel_id=1, source_target_pairs={{0,12},{1,13},{2,14},{3,15},{4,8},{5,9},{6,10},{7,11},{8,4},{9,5},... | collective-permute-start | bytes 393224 | tf_op jit(solution)/shard_map/ppermute | solution.py:42
  155.2 11.2 %collective-permute-start.39 = (bf16[8,2048]{1,0:T(8,128)(2,1)S(1)}, bf16[8,2048]{1,0:T(8,128)(2,1)S(1)}, u32[]{:S(2)}, u32[]{:S(2)}) collective-permute-start(bf16[8,2048]{1,0:T(8,128)(2,1)S(1)} %get-tuple-element.39), channel_id=1, source_target_pairs={{0,1},{1,2},{2,3},{3,4},{4,5},{5,6},{6,7},{7,8},{8,9},{9,10},{10,1... | collective-permute-start | bytes 98312 | tf_op jit(solution)/shard_map/ppermute | solution.py:42
  157.8 19.6 %collective-permute-start.43 = (bf16[128,512]{1,0:T(8,128)(2,1)S(1)}, bf16[128,512]{1,0:T(8,128)(2,1)S(1)}, u32[]{:S(2)}, u32[]{:S(2)}) collective-permute-start(bf16[128,512]{1,0:T(8,128)(2,1)S(1)} %get-tuple-element.38), channel_id=1, source_target_pairs={{0,4},{1,5},{2,6},{3,7},{4,0},{5,1},{6,2},{7,3},{8,12},{9,13},{10,... | collective-permute-start | bytes 393224 | tf_op jit(solution)/shard_map/ppermute | solution.py:42
  163.8 14.0 %collective-permute-start.45 = (bf16[128,512]{1,0:T(8,128)(2,1)S(1)}, bf16[128,512]{1,0:T(8,128)(2,1)S(1)}, u32[]{:S(2)}, u32[]{:S(2)}) collective-permute-start(bf16[128,512]{1,0:T(8,128)(2,1)S(1)} %get-tuple-element.35), channel_id=1, source_target_pairs={{0,8},{1,9},{2,10},{3,11},{4,12},{5,13},{6,14},{7,15},{8,0},{9,1},... | collective-permute-start | bytes 393224 | tf_op jit(solution)/shard_map/ppermute | solution.py:42
  165.0 12.9 %collective-permute-start.44 = (bf16[128,512]{1,0:T(8,128)(2,1)S(1)}, bf16[128,512]{1,0:T(8,128)(2,1)S(1)}, u32[]{:S(2)}, u32[]{:S(2)}) collective-permute-start(bf16[128,512]{1,0:T(8,128)(2,1)S(1)} %get-tuple-element.36), channel_id=1, source_target_pairs={{0,12},{1,13},{2,14},{3,15},{4,8},{5,9},{6,10},{7,11},{8,4},{9,5},... | collective-permute-start | bytes 393224 | tf_op jit(solution)/shard_map/ppermute | solution.py:42
  171.3 31.1 %collective-permute-start.41 = (bf16[128,2048]{1,0:T(8,128)(2,1)S(1)}, bf16[128,2048]{1,0:T(8,128)(2,1)S(1)}, u32[]{:S(2)}, u32[]{:S(2)}) collective-permute-start(bf16[128,2048]{1,0:T(8,128)(2,1)S(1)} %get-tuple-element.14), channel_id=1, source_target_pairs={{16,0},{17,1},{18,2},{19,3},{20,4},{21,5},{22,6},{23,7},{24,8},{25... | collective-permute-start | bytes 1572872 | tf_op jit(solution)/shard_map/ppermute | solution.py:42
  172.6 17.7 %collective-permute-start.42 = (bf16[144,2048]{1,0:T(8,128)(2,1)S(1)}, bf16[144,2048]{1,0:T(8,128)(2,1)S(1)}, u32[]{:S(2)}, u32[]{:S(2)}) collective-permute-start(bf16[144,2048]{1,0:T(8,128)(2,1)S(1)} %pad_maximum_fusion.4), channel_id=1, source_target_pairs={{0,16},{1,17},{2,18},{3,19},{4,20},{5,21},{6,22},{7,23},{8,24},{9,... | collective-permute-start | bytes 1769480 | tf_op jit(solution)/shard_map/ppermute | solution.py:42
  177.8 11.8 %collective-permute-start.48 = (bf16[2,128,512]{2,1,0:T(8,128)(2,1)S(1)}, bf16[2,128,512]{2,1,0:T(8,128)(2,1)S(1)}, u32[]{:S(2)}, u32[]{:S(2)}) collective-permute-start(bf16[2,128,512]{2,1,0:T(8,128)(2,1)S(1)} %maximum_select_fusion.16), channel_id=1, source_target_pairs={{0,1},{1,0},{2,3},{3,2},{4,5},{5,4},{6,7},{7,6},{8,9},{9,8},{10,11... | collective-permute-start | bytes 786440 | tf_op jit(solution)/shard_map/ppermute | solution.py:42
  177.9 11.8 %collective-permute-start.47 = (bf16[2,128,512]{2,1,0:T(8,128)(2,1)S(1)}, bf16[2,128,512]{2,1,0:T(8,128)(2,1)S(1)}, u32[]{:S(2)}, u32[]{:S(2)}) collective-permute-start(bf16[2,128,512]{2,1,0:T(8,128)(2,1)S(1)} %maximum_select_fusion.17), channel_id=1, source_target_pairs={{0,2},{1,3},{2,0},{3,1},{4,6},{5,7},{6,4},{7,5},{8,10},{9,11},{10,... | collective-permute-start | bytes 786440 | tf_op jit(solution)/shard_map/ppermute | solution.py:42
  197.8 13.0 %collective-permute-start.54 = (bf16[128,512]{0,1:T(8,128)(2,1)S(1)}, bf16[128,512]{0,1:T(8,128)(2,1)S(1)}, u32[]{:S(2)}, u32[]{:S(2)}) collective-permute-start(bf16[128,512]{0,1:T(8,128)(2,1)S(1)} %get-tuple-element.31), channel_id=1, source_target_pairs={{0,8},{1,9},{2,10},{3,11},{4,12},{5,13},{6,14},{7,15},{8,0},{9,1},... | collective-permute-start | bytes 393224 | tf_op jit(solution)/shard_map/ppermute | solution.py:42
  199.8 11.0 %collective-permute-start.53 = (bf16[128,512]{0,1:T(8,128)(2,1)S(1)}, bf16[128,512]{0,1:T(8,128)(2,1)S(1)}, u32[]{:S(2)}, u32[]{:S(2)}) collective-permute-start(bf16[128,512]{0,1:T(8,128)(2,1)S(1)} %get-tuple-element.32), channel_id=1, source_target_pairs={{0,12},{1,13},{2,14},{3,15},{4,8},{5,9},{6,10},{7,11},{8,4},{9,5},... | collective-permute-start | bytes 393224 | tf_op jit(solution)/shard_map/ppermute | solution.py:42
  (34 other events, 250.8 us)
